TPU v7x, 512 devices: a whole 4x8x8 slice. The times are simulated.
512 devices in a mesh: blk: 64 (over x, z_hi, y), grp: 8 (over z_lo, core).
Axes of the slice: x: 4, y: 8, z: 8 (z_hi: 2, z_lo: 4; z = z_hi * 4 + z_lo), core: 2. Of those that a mesh axis runs over, the one named last changes fastest.
Arguments:
- excitation: bfloat16 [128, 1024, 256], P('blk'), may hold values from -6 to 6
- inverse_self: bfloat16 [128, 1024, 1024], P('blk', 'grp'), may hold values from -0.1875 to 0.1875
- coupling: bfloat16 [128, 4, 1024, 1024], P('blk', None, 'grp'), may hold values from -0.1875 to 0.1875
- neighbour_mask: int32 [128, 4], P('blk'), may hold values 0 or 1
- sketch: float32 [5, 256, 32], replicated, may hold values from -6 to 6
Outputs:
- bases: float32 [128, 1024, 32], P('blk', 'grp')
- reduced_coupling: float32 [128, 4, 32, 32], P('blk')
- reduced_excitation: float32 [128, 32, 256], P('blk')
Inputs may be any that keep to these rules, and one draw needn't show every extreme that they name: `neighbour_mask`: 1 where the block at that slot's offset adds secondary currents, 0 where it does not; slots pointing outside the array add nothing in any case.
All inputs are finite; a program needn't handle non-finite values.
Results may differ from a plain program's by a relative error of at most 0.0003.
Values sent between devices are 32-bit elements; how exact they have to be, the bound alone decides.
No kernel may reach another device: no remote copies, remote signals or barrier semaphores. Data moves between devices by JAX's collectives and lax.ppermute only.
A program may use at most 64 MiB of HBM per device.

v0:
```python
import math

import jax
import jax.numpy as jnp
from jax import lax
from jax.sharding import PartitionSpec as P

neighbour_offsets = (-2, -1, 1, 2)


def extended(array, sides, width):
    for axis, dim in sides:
        size, length = (lax.axis_size(axis), array.shape[dim])
        up = [(i, (i + 1) % size) for i in range(size - 1)]
        down = [(j, i) for i, j in up]
        last = lax.slice_in_dim(array, length - width, length, axis=dim)
        initial = lax.slice_in_dim(array, 0, width, axis=dim)
        before = lax.ppermute(last, axis, up)
        after = lax.ppermute(initial, axis, down)
        array = jnp.concatenate([before, array, after], axis=dim)
    return array


def exact_einsum(form, left, right):
    return jnp.einsum(
        form, left, right, precision=lax.Precision.HIGHEST, preferred_element_type=jnp.float32
    )


def shards(excitation, inverse_self, coupling, neighbour_mask, sketch):
    blocks, unknowns, columns = excitation.shape
    shard_rows = inverse_self.shape[1]
    retained = sketch.shape[2]
    row_start = lax.axis_index("grp") * shard_rows
    own_excitation = lax.dynamic_slice_in_dim(excitation, row_start, shard_rows, 1)
    primary = jnp.einsum(
        "bnm,bmp->bnp", inverse_self, excitation, preferred_element_type=jnp.float32
    )
    weights_mask = neighbour_mask.astype(jnp.float32)
    own_whole = lax.all_gather(primary, "grp", axis=1, tiled=True)
    nearby = extended(own_whole, (("blk", 0),), 2)
    sources = jnp.zeros((blocks, shard_rows, retained), jnp.float32)
    for slot_index, offset in enumerate(neighbour_offsets):
        neighbour = nearby[2 + offset : 2 + offset + blocks]
        coupled_full = exact_einsum("bnm,bmp->bnp", coupling[:, slot_index], neighbour)
        coupled_term = exact_einsum("bnp,pr->bnr", coupled_full, sketch[slot_index + 1])
        sources = sources + weights_mask[:, slot_index, None, None] * coupled_term
    all_sources = lax.all_gather(sources, "grp", axis=1, tiled=True)
    sketched = exact_einsum("bnp,pr->bnr", primary, sketch[0]) - exact_einsum(
        "bnm,bmr->bnr", inverse_self, all_sources
    )
    gram_part = exact_einsum("bnr,bns->brs", sketched, sketched)
    gram_total = lax.psum(gram_part, "grp") / unknowns
    chol_lower = jnp.linalg.cholesky(gram_total)
    bases = lax.linalg.triangular_solve(
        chol_lower, sketched, left_side=False, lower=True, transpose_a=True
    )
    basis_shards = extended(bases, (("blk", 0),), 2)
    basis_near = lax.all_gather(basis_shards, "grp", axis=1, tiled=True)
    stacked = []
    for slot_index, offset in enumerate(neighbour_offsets):
        coupled_basis = exact_einsum(
            "bnm,bmr->bnr", coupling[:, slot_index], basis_near[2 + offset : 2 + offset + blocks]
        )
        stacked.append(exact_einsum("bnr,bns->brs", bases, coupled_basis))
    coupled_part = jnp.stack(stacked, axis=1)
    driven_part = exact_einsum("bnr,bnp->brp", bases, own_excitation)
    coupled_sum, driven_sum = lax.psum((coupled_part, driven_part), "grp")
    norm_scale = 1.0 / math.sqrt(unknowns)
    return (bases, coupled_sum * norm_scale, driven_sum * norm_scale)


def solution(mesh):
    return jax.shard_map(
        shards,
        mesh=mesh,
        in_specs=(
            P("blk", None, None),
            P("blk", "grp", None),
            P("blk", None, "grp", None),
            P("blk", None),
            P(),
        ),
        out_specs=(P("blk", "grp", None), P("blk", None, None, None), P("blk", None, None)),
        check_vma=False,
    )
```

profile of v0, /device:TPU:7, one launch (start us, length us, event | category | flops | bytes accessed | tf_op | source)
XLA Modules:
  0.0 312.9 jit_solution(14222659182359712413)
XLA Ops:
  7.3 1.1 copy-done
  8.4 2.1 fusion.57
  10.5 45.0 %all-gather.2.cloned.1.call-done = f32[2,1024,256]{2,1,0:T(8,128)} async-done(((f32[2,128,256]{2,1,0:T(8,128)}), f32[2,1024,256]{2,1,0:T(8,128)}) %all-gather.2.cloned.1.call-update) | async-done | bytes 2097168 | tf_op jit(solution)/shard_map/all_gather | solution.py:40
  55.5 3.1 collective-permute-start
  58.6 9.1 %collective-permute-start.1 = (f32[2,1024,256]{2,1,0:T(8,128)}, f32[2,1024,256]{2,1,0:T(8,128)}, u32[]{:S(2)}, u32[]{:S(2)}) collective-permute-start(f32[2,1024,256]{2,1,0:T(8,128)} %all-gather.2.cloned.1.call-done), channel_id=1, source_target_pairs={{8,0},{16,8},{24,16},{32,24},{40,32},{48,40},{56,48},{64,56},{72,6... | collective-permute-start | bytes 6291464 | tf_op jit(solution)/shard_map/ppermute | solution.py:19
  68.0 1.4 fusion.47
  69.5 85.0 %collective-permute-done = f32[2,1024,256]{2,1,0:T(8,128)} collective-permute-done((f32[2,1024,256]{2,1,0:T(8,128)}, f32[2,1024,256]{2,1,0:T(8,128)}, u32[]{:S(2)}, u32[]{:S(2)}) %collective-permute-start) | collective-permute-done | bytes 2097184 | tf_op jit(solution)/shard_map/ppermute | solution.py:18
  154.5 3.4 %convolution_bitcast_fusion.1 = f32[2,128,256]{1,2,0:T(8,128)S(1)} fusion(f32[2,1024,256]{2,1,0:T(8,128)} %collective-permute-done, bf16[2,4,128,1024]{3,2,1,0:T(8,128)(2,1)S(1)} %copy-done.1), kind=kOutput, calls=%fused_computation.11 | convolution fusion | flops 805306368 | bytes 2883584 | tf_op jit(solution)/shard_map/bnm,bmp->bnp/dot_general | solution.py:25
  158.2 3.0 fusion.11
  161.2 0.3 fusion.17
  161.5 3.0 fusion.8
  164.8 3.4 %convolution_bitcast_fusion = f32[2,128,256]{1,2,0:T(8,128)S(1)} fusion(f32[2,1024,256]{2,1,0:T(8,128)} %collective-permute-done.1, bf16[2,4,128,1024]{3,2,1,0:T(8,128)(2,1)S(1)} %copy-done.1), kind=kOutput, calls=%fused_computation.10 | convolution fusion | flops 805306368 | bytes 2883584 | tf_op jit(solution)/shard_map/bnm,bmp->bnp/dot_general | solution.py:25
  168.3 0.3 fusion.15
  168.5 17.3 %all_gather.10 = f32[2,1024,32]{1,2,0:T(8,128)S(1)} all-gather(f32[2,128,32]{1,2,0:T(8,128)S(1)} %fusion.15), channel_id=1, replica_groups=mesh['blk'=64,'grp'=8] {'grp'}, dimensions={1}, use_global_device_ids=true | all-gather | bytes 294912 | tf_op jit(solution)/shard_map/all_gather | solution.py:48
  185.8 0.6 fusion.14
  186.6 22.2 %psum.21 = f32[2,32,32]{1,2,0:T(8,128)S(1)} all-reduce(f32[2,32,32]{1,2,0:T(8,128)S(1)} %fusion.58), channel_id=1, replica_groups=mesh['blk'=64,'grp'=8] {'grp'}, use_global_device_ids=true, to_apply=%region_0.0 | all-reduce | flops 2048 | bytes 16384 | tf_op jit(solution)/shard_map/psum | solution.py:53
  208.9 5.9 %custom-call.7 = f32[2,32,32]{2,1,0:T(8,128)S(1)} custom-call(f32[2,32,32]{2,1,0:T(8,128)S(1)} %fusion.42), custom_call_target="Cholesky" | custom-call | tf_op jit(solution)/shard_map/jit(cholesky)/cholesky | solution.py:54
  215.0 4.9 %custom-call.8 = f32[2,1,32,32]{2,3,1,0:T(8,128)S(1)} custom-call(f32[2,1,32,32]{3,2,1,0:T(8,128)S(1)} %select_bitcast_fusion), custom_call_target="InvertDiagBlocksLowerTriangular" | custom-call | tf_op jit(solution)/shard_map/triangular_solve | solution.py:55
  219.9 0.3 fusion.40
  220.2 5.2 %collective-permute-start.3 = (f32[2,128,32]{1,2,0:T(8,128)S(1)}, f32[2,128,32]{1,2,0:T(8,128)S(1)}, u32[]{:S(2)}, u32[]{:S(2)}) collective-permute-start(f32[2,128,32]{1,2,0:T(8,128)S(1)} %fusion.40), channel_id=1, source_target_pairs={{8,0},{16,8},{24,16},{32,24},{40,32},{48,40},{56,48},{64,56},{72,6... | collective-permute-start | bytes 98312 | tf_op jit(solution)/shard_map/ppermute | solution.py:19
  225.4 1.9 collective-permute-start.2
  227.3 0.8 fusion.38
  228.2 8.8 %collective-permute-done.2 = f32[2,128,32]{1,2,0:T(8,128)S(1)} collective-permute-done((f32[2,128,32]{1,2,0:T(8,128)S(1)}, f32[2,128,32]{1,2,0:T(8,128)S(1)}, u32[]{:S(2)}, u32[]{:S(2)}) %collective-permute-start.2) | collective-permute-done | bytes 32800 | tf_op jit(solution)/shard_map/ppermute | solution.py:18
  237.0 21.3 %all_gather.11 = f32[6,1024,32]{1,2,0:T(8,128)S(1)} all-gather(f32[6,128,32]{1,2,0:T(8,128)S(1)} %pad_maximum_fusion.1), channel_id=1, replica_groups=mesh['blk'=64,'grp'=8] {'grp'}, dimensions={1}, use_global_device_ids=true | all-gather | bytes 884736 | tf_op jit(solution)/shard_map/all_gather | solution.py:59
  258.3 0.6 fusion.18
  258.9 0.6 fusion.21
  259.5 0.6 fusion.24
  260.1 0.6 fusion.27
  261.5 24.1 %psum.22 = f32[2,4,32,32]{3,2,0,1:T(8,128)S(1)} all-reduce(f32[2,4,32,32]{3,2,0,1:T(8,128)S(1)} %pad_maximum_fusion), channel_id=1, replica_groups=mesh['blk'=64,'grp'=8] {'grp'}, use_global_device_ids=true, to_apply=%region_3.4 | all-reduce | flops 8192 | bytes 65536 | tf_op jit(solution)/shard_map/psum | solution.py:68
  285.6 0.7 copy.15
  286.2 18.3 %all-reduce.2.cloned.1.call-done = f32[2,32,256]{2,1,0:T(8,128)} async-done(((f32[2,32,256]{2,1,0:T(8,128)}), f32[2,32,256]{2,1,0:T(8,128)}) %all-reduce.2.cloned.1.call-update) | async-done | bytes 65552 | tf_op jit(solution)/shard_map/psum | solution.py:68
  304.6 1.5 broadcast_multiply_fusion.1
  (39 shorter events, 2.1 us)
Async XLA Ops:
  7.2 1.2 copy-start
  7.2 60.6 %copy-start.6 = (s32[2,4]{1,0:T(2,128)S(1)}, s32[2,4]{1,0:T(2,128)}, u32[]{:S(2)}) copy-start(s32[2,4]{1,0:T(2,128)} %param.8) | copy-start | bytes 100
  7.2 60.8 %copy-start.5 = (f32[5,256,32]{1,2,0:T(8,128)S(1)}, f32[5,256,32]{1,2,0:T(8,128)}, u32[]{:S(2)}) copy-start(f32[5,256,32]{1,2,0:T(8,128)} %param.9) | copy-start | bytes 491524
  7.2 147.3 %copy-start.1 = (bf16[2,4,128,1024]{3,2,1,0:T(8,128)(2,1)S(1)}, bf16[2,4,128,1024]{3,2,1,0:T(8,128)(2,1)}, u32[]{:S(2)}) copy-start(bf16[2,4,128,1024]{3,2,1,0:T(8,128)(2,1)} %param.7) | copy-start | bytes 6291460
  7.2 48.3 %all-gather.2.cloned.1.call-start = ((), (), s32[]{:S(2)}) async-start(), calls=%async_computation | async-start | bytes 2359296 | tf_op jit(solution)/shard_map/all_gather | solution.py:40
  10.5 294.1 %all-reduce.2.cloned.1.call-start = ((), (), s32[]{:S(2)}) async-start(), calls=%async_computation.1 | async-start | bytes 131072 | tf_op jit(solution)/shard_map/psum | solution.py:68
  55.5 98.9 %collective-permute-start = (f32[2,1024,256]{2,1,0:T(8,128)}, f32[2,1024,256]{2,1,0:T(8,128)}, u32[]{:S(2)}, u32[]{:S(2)}) collective-permute-start(f32[2,1024,256]{2,1,0:T(8,128)} %all-gather.2.cloned.1.call-done), channel_id=1, source_target_pairs={{0,8},{8,16},{16,24},{24,32},{32,40},{40,48},{48,56},{56,64},{64,7... | collective-permute-start | bytes 6291464 | tf_op jit(solution)/shard_map/ppermute | solution.py:18
  58.6 102.9 %collective-permute-start.1 = (f32[2,1024,256]{2,1,0:T(8,128)}, f32[2,1024,256]{2,1,0:T(8,128)}, u32[]{:S(2)}, u32[]{:S(2)}) collective-permute-start(f32[2,1024,256]{2,1,0:T(8,128)} %all-gather.2.cloned.1.call-done), channel_id=1, source_target_pairs={{8,0},{16,8},{24,16},{32,24},{40,32},{48,40},{56,48},{64,56},{72,6... | collective-permute-start | bytes 6291464 | tf_op jit(solution)/shard_map/ppermute | solution.py:19
  67.8 90.4 %copy-start.2 = (f32[2,1024,256]{2,1,0:T(8,128)S(1)}, f32[2,1024,256]{2,1,0:T(8,128)}, u32[]{:S(2)}) copy-start(f32[2,1024,256]{2,1,0:T(8,128)} %all-gather.2.cloned.1.call-done) | copy-start | bytes 6291460
  164.6 21.3 %copy-start.3 = (bf16[2,128,1024]{2,1,0:T(8,128)(2,1)S(1)}, bf16[2,128,1024]{2,1,0:T(8,128)(2,1)}, u32[]{:S(2)}) copy-start(bf16[2,128,1024]{2,1,0:T(8,128)(2,1)} %param.6) | copy-start | bytes 1572868
  220.2 41.1 %copy-start.4 = (f32[2,128,32]{1,2,0:T(8,128)}, f32[2,128,32]{1,2,0:T(8,128)S(1)}, u32[]{:S(2)}) copy-start(f32[2,128,32]{1,2,0:T(8,128)S(1)} %fusion.40) | copy-start | bytes 98308
  220.2 7.9 %collective-permute-start.3 = (f32[2,128,32]{1,2,0:T(8,128)S(1)}, f32[2,128,32]{1,2,0:T(8,128)S(1)}, u32[]{:S(2)}, u32[]{:S(2)}) collective-permute-start(f32[2,128,32]{1,2,0:T(8,128)S(1)} %fusion.40), channel_id=1, source_target_pairs={{8,0},{16,8},{24,16},{32,24},{40,32},{48,40},{56,48},{64,56},{72,6... | collective-permute-start | bytes 98312 | tf_op jit(solution)/shard_map/ppermute | solution.py:19
  225.4 11.6 %collective-permute-start.2 = (f32[2,128,32]{1,2,0:T(8,128)S(1)}, f32[2,128,32]{1,2,0:T(8,128)S(1)}, u32[]{:S(2)}, u32[]{:S(2)}) collective-permute-start(f32[2,128,32]{1,2,0:T(8,128)S(1)} %fusion.40), channel_id=1, source_target_pairs={{0,8},{8,16},{16,24},{24,32},{32,40},{40,48},{48,56},{56,64},{64,7... | collective-permute-start | bytes 98312 | tf_op jit(solution)/shard_map/ppermute | solution.py:18
Sparse Core Ops, SparseCore 0:
  10.6 44.8 all-gather.1
  228.3 76.2 all-reduce.1
where the time goes:
time: 316 us; the launch traced here: 313 us
  waiting for transfers between devices  157 us (50%)
  blocking collectives  84.9 us (27%)
  matrix products  22.4 us (7%)
  starting transfers between devices  19.4 us (6%)
  between operations  14.4 us (5%)
  other arithmetic  12.6 us (4%)
    ppermute x2, waiting for transfers between devices, extended(): before = lax.ppermute(last, axis, up)  93.8 us
    all_gather x1, waiting for transfers between devices, shards(): own_whole = lax.all_gather(primary, 'grp', axis=1, tiled=True)  45 us
    psum x1, blocking collectives, shards(): coupled_sum, driven_sum = lax.psum((coupled_part, driven_part), 'grp')  24.1 us
    psum x1, blocking collectives, shards(): gram_total = lax.psum(gram_part, 'grp') / unknowns  22.2 us
    all_gather x1, blocking collectives, shards(): basis_near = lax.all_gather(basis_shards, 'grp', axis=1, tiled=True)  21.3 us
    dot_general x20, matrix products, exact_einsum(): jnp.einsum(form, left, right, precision=lax.Precision.HIGHEST, preferred_...  20.1 us
    psum x1, waiting for transfers between devices, shards(): coupled_sum, driven_sum = lax.psum((coupled_part, driven_part), 'grp')  18.3 us
    all_gather x1, blocking collectives, shards(): all_sources = lax.all_gather(sources, 'grp', axis=1, tiled=True)  17.3 us
  transfers between devices with their start and end apart: 6, of which 4 were waited for; matrix products, arithmetic and copies ran while one was open for 4% of the time, Pallas kernels for 0%

commit v1 on v0

v1 whole, which is shorter than its diff:
```python
import functools

import jax
import jax.numpy as jnp
from jax import lax
from jax.experimental import pallas as pl
from jax.experimental.pallas import tpu as pltpu
from jax.sharding import PartitionSpec as P

F32, BF16 = jnp.float32, jnp.bfloat16
NT = (((1,), (1,)), ((), ()))
NN = (((1,), (0,)), ((), ()))
chip_groups = [[0, 2, 4, 6], [1, 3, 5, 7]]
core_groups = [[0, 1], [2, 3], [4, 5], [6, 7]]


def halves(value):
    high = value.astype(BF16)
    return high, (value - high.astype(F32)).astype(BF16)


def stacked_halves(value):
    return jnp.concatenate(halves(value), axis=0)


def dot(left, right, dims):
    return lax.dot_general(left, right, dims, preferred_element_type=F32)


def folded(left, right, dims):
    rows = left.shape[0]
    both = dot(stacked_halves(left), right, dims)
    return both[:rows] + both[rows:]


def exact(left, right, dims):
    rows = left.shape[0]
    right_high, right_low = halves(right)
    left_high, left_low = halves(left)
    both = dot(jnp.concatenate([left_high, left_low], axis=0), right_high, dims)
    return both[:rows] + (both[rows:] + dot(left_high, right_low, dims))


def call(kernel, outs, *, scratch=(), smem=0, vmem=32):
    def run(*args):
        specs = [pl.BlockSpec(memory_space=pltpu.SMEM)] * smem
        specs += [pl.BlockSpec(memory_space=pltpu.VMEM)] * (len(args) - smem)
        return pl.pallas_call(
            kernel,
            out_shape=[jax.ShapeDtypeStruct(shape, F32) for shape in outs],
            in_specs=specs,
            out_specs=[pl.BlockSpec(memory_space=pltpu.VMEM)] * len(outs),
            scratch_shapes=list(scratch),
            compiler_params=pltpu.CompilerParams(vmem_limit_bytes=vmem << 20),
        )(*args)

    return run


def primary_kernel(place, exc, inv, sk, own, local, first, second):
    parity = place[0]
    rows = []
    for i in range(2):
        primary = dot(inv[i], exc[i], NN)
        rows.append(exact(sk[...], primary, NT))
        own[i] = rows[i][0:32]
    part = lambda i, k: rows[i][32 * k : 32 * k + 32]
    local[0] = part(1, 3)
    local[1] = part(0, 2)
    up = [part(0, 1), part(1, 1), part(1, 2)]
    down = [part(0, 4), part(1, 4), part(0, 3)]
    even = parity == 0
    for n in range(3):
        first[n] = jnp.where(even, up[n], down[n])
        second[n] = jnp.where(even, down[n], up[n])


def sources_kernel(place, mask, same, other, coup, out, high, low):
    parity, core = place[0], place[1]
    for z in range(4):
        for piece in range(8):
            for src, c in ((same, core), (other, 1 - core)):
                h, l = halves(src[z, piece])
                high[2 * z + c, piece] = h
                low[2 * z + c, piece] = l

    def piece_of(n):
        return jnp.concatenate(
            [
                jnp.concatenate([high[g, n] for g in range(8)], axis=1),
                jnp.concatenate([low[g, n] for g in range(8)], axis=1),
            ],
            axis=0,
        )

    before = 5 - 3 * parity
    after = 2 + 3 * parity
    table = (
        (before, before + 2, 0, after),
        (before + 1, 1, after + 2, after + 1),
    )
    for i in range(2):
        total = jnp.zeros((32, 128), F32)
        for k in range(4):
            both = dot(piece_of(table[i][k]), coup[i, k], NT)
            total = total + mask[i, k].astype(F32) * (both[:32] + both[32:])
        for z in range(4):
            out[z, i] = total


def sketched_kernel(own, src, inv, out):
    for i in range(2):
        whole = jnp.concatenate([src[g % 2, g // 2, i] for g in range(8)], axis=1)
        out[i] = own[i] - folded(whole, inv[i], NT)


def lower_inverse(gram):
    n = gram.shape[0]
    row = lax.broadcasted_iota(jnp.int32, (n, 32, 32), 1)
    col = lax.broadcasted_iota(jnp.int32, (n, 32, 32), 2)
    inverse = jnp.where(row == col, 1.0, 0.0).astype(F32)
    work = gram
    for j in range(32):
        scale = lax.rsqrt(work[:, j : j + 1, j : j + 1])
        pivot = work[:, j : j + 1, :] * scale
        pivot_inverse = inverse[:, j : j + 1, :] * scale
        factor = work[:, :, j : j + 1] * scale
        below = jnp.where(row[:, :, 0:1] > j, factor, 0.0)
        at = row == j
        inverse = jnp.where(at, pivot_inverse, inverse - below * pivot_inverse)
        work = work - below * pivot
    return inverse


def reduce_kernel(place, near, mine, exc, coup, bases, coupled, driven):
    parity = place[0]
    whole = []
    grams = []
    for n in range(6):
        w = jnp.concatenate([near[g, n] for g in range(8)], axis=1)
        whole.append(w)
        grams.append(
            lax.dot_general(
                w, w, NT, precision=lax.Precision.HIGHEST, preferred_element_type=F32
            )
            * (1.0 / 1024)
        )
    diagonal = lax.broadcasted_iota(jnp.int32, (32, 32), 0) == lax.broadcasted_iota(
        jnp.int32, (32, 32), 1
    )
    absent = jnp.where(diagonal, 1.0 - place[2].astype(F32), 0.0)
    grams[4] = grams[4] + absent
    grams[5] = grams[5] + absent
    inverse = lower_inverse(jnp.stack(grams))
    full = [exact(inverse[n], whole[n], NN) for n in range(6)]
    even = parity == 0
    before = [jnp.where(even, full[4 + n], full[2 + n]) for n in range(2)]
    after = [jnp.where(even, full[2 + n], full[4 + n]) for n in range(2)]
    line = [before[0], before[1], full[0], full[1], after[0], after[1]]
    for i in range(2):
        part = exact(inverse[i], mine[i], NN)
        bases[i] = part.T
        driven[i] = folded(full[i], exc[i], NN) * (1.0 / 32)
        stack = []
        for k, o in enumerate((-2, -1, 1, 2)):
            stack.append(folded(line[2 + i + o], coup[i, k], NT))
        value = exact(part, jnp.concatenate(stack, axis=0), NT) * (1.0 / 32)
        for z in range(4):
            coupled[z, i] = value


def sum_kernel(parts, out):
    total = parts[0, 0]
    for g in range(1, 8):
        total = total + parts[g % 2, g // 2]
    for i in range(2):
        for k in range(4):
            out[i, k] = total[i, :, 32 * k : 32 * k + 32]


def exchange(first, second):
    size = lax.axis_size("blk")

    def pairs(start):
        ups = [(i, i + 1) for i in range(start, size - 1, 2)]
        return ups + [(j, i) for i, j in ups]

    got_second = lax.ppermute(second, "blk", pairs(1))
    got_first = lax.ppermute(first, "blk", pairs(0))
    return got_first, got_second


def share(value):
    over_chips = lax.all_to_all(value, "grp", 0, 0, axis_index_groups=chip_groups)
    return lax.all_gather(over_chips, "grp", axis=0, axis_index_groups=core_groups)


def shards(excitation, inverse_self, coupling, neighbour_mask, sketch):
    block_at, member = lax.axis_index("blk"), lax.axis_index("grp")
    inner = (block_at > 0) & (block_at < lax.axis_size("blk") - 1)
    place = jnp.stack([block_at % 2, member % 2, inner.astype(jnp.int32)])
    turned = sketch.transpose(0, 2, 1).reshape(160, 256)
    own, local, first, second = call(
        primary_kernel, [(2, 32, 128), (2, 32, 128), (3, 32, 128), (3, 32, 128)], smem=1
    )(place, excitation, inverse_self, turned)
    got_first, got_second = exchange(first, second)
    pieces = jnp.concatenate([local, got_first, got_second], axis=0)
    same = lax.all_gather(pieces, "grp", axis=0, axis_index_groups=chip_groups)
    other = lax.ppermute(same, "grp", [(g, g ^ 1) for g in range(8)])
    (sources,) = call(
        sources_kernel,
        [(4, 2, 32, 128)],
        smem=2,
        scratch=[pltpu.VMEM((8, 8, 32, 128), BF16), pltpu.VMEM((8, 8, 32, 128), BF16)],
    )(place, neighbour_mask, same, other, coupling)
    (sketched,) = call(sketched_kernel, [(2, 32, 128)])(own, share(sources), inverse_self)
    got_first, got_second = exchange(sketched, sketched)
    near = lax.all_gather(
        jnp.concatenate([sketched, got_first, got_second], axis=0), "grp", axis=0
    )
    bases, coupled, driven = call(
        reduce_kernel, [(2, 128, 32), (4, 2, 32, 128), (2, 32, 256)], smem=1
    )(place, near, sketched, excitation, coupling)
    (reduced,) = call(sum_kernel, [(2, 4, 32, 32)])(share(coupled))
    return bases, reduced, driven


def solution(mesh):
    return jax.shard_map(
        shards,
        mesh=mesh,
        in_specs=(
            P("blk", None, None),
            P("blk", "grp", None),
            P("blk", None, "grp", None),
            P("blk", None),
            P(),
        ),
        out_specs=(P("blk", "grp", None), P("blk", None, None, None), P("blk", None, None)),
        check_vma=False,
    )
```

time: 316 us -> 111 us (0.35)
  waiting for transfers between devices: 157 us -> 10.3 us
  blocking collectives: 84.9 us -> 46.6 us
  matrix products: 22.4 us -> 0 us
  starting transfers between devices: 19.4 us -> 38.5 us
  between operations: 14.4 us -> 0.77 us
  other arithmetic: 12.6 us -> 0.09 us
  Pallas kernels: 0 us -> 10.3 us
    ppermute x4 -> x5, waiting for transfers between devices: 93.8 us -> 6.2 us  [the longest x2 2.72 us: exchange(): got_first = lax.ppermute(first, 'blk', pairs(0))]
    psum x2 -> x0, blocking collectives: 46.3 us -> none  [the longest x1 24.1 us: shards(): coupled_sum, driven_sum = lax.psum((coupled_part, driven_part), 'grp')]
    all_gather x1 -> x0, waiting for transfers between devices: 45 us -> none  [shards(): own_whole = lax.all_gather(primary, 'grp', axis=1, tiled=True)]
    dot_general x21 -> x0, matrix products: 22.2 us -> none  [the longest x20 20.1 us: exact_einsum(): jnp.einsum(form, left, right, precision=lax.Precision.HIGHEST, preferred_...]
    psum x1 -> x0, waiting for transfers between devices: 18.3 us -> none  [shards(): coupled_sum, driven_sum = lax.psum((coupled_part, driven_part), 'grp')]
    ppermute x4 -> x5, starting transfers between devices: 19.3 us -> 35.2 us  [the longest x2 24 us: exchange(): got_second = lax.ppermute(second, 'blk', pairs(1))]
    another operation x8 -> x1, other arithmetic: 11 us -> 0.08 us  [shards(): place = jnp.stack([block_at % 2, member % 2, inner.astype(jnp.int32)])]
    pallas_call x0 -> x5, Pallas kernels: none -> 10.3 us  [run(): pl.pallas_call(kernel, out_shape=[jax.ShapeDtypeStruct(shape, F32) for sh...]
  transfers between devices with their start and end apart: 6 -> 6, of which waited for: 4 -> 4; matrix products, arithmetic and copies ran while one was open for 4% -> 1% of each run, Pallas kernels for 0% -> 0%
where the time goes in v1:
time: 111 us
  blocking collectives  46.6 us (42%)
  starting transfers between devices  38.5 us (35%)
  Pallas kernels  10.3 us (9%)
  waiting for transfers between devices  10.3 us (9%)
  local copies, waits for them, and re-layouts  4.02 us (4%)
    ppermute x2, starting transfers between devices, exchange(): got_second = lax.ppermute(second, 'blk', pairs(1))  24 us
    all_gather x1, blocking collectives, shards(): lax.all_gather(jnp.concatenate([sketched, got_first, got_second], axis=0)...  17.3 us
    all_gather x1, blocking collectives, shards(): same = lax.all_gather(pieces, 'grp', axis=0, axis_index_groups=chip_groups)  13.4 us
    pallas_call x5, Pallas kernels, run(): pl.pallas_call(kernel, out_shape=[jax.ShapeDtypeStruct(shape, F32) for sh...  10.3 us
    all_to_all x1, blocking collectives, share(): lax.all_to_all(value, 'grp', 0, 0, axis_index_groups=chip_groups)  8.79 us
    all_gather x2, blocking collectives, share(): lax.all_gather(over_chips, 'grp', axis=0, axis_index_groups=core_groups)  7.11 us
    ppermute x1, starting transfers between devices, shards(): other = lax.ppermute(same, 'grp', [(g, g ^ 1) for g in range(8)])  6.13 us
    ppermute x2, starting transfers between devices, exchange(): got_first = lax.ppermute(first, 'blk', pairs(0))  5.13 us
  transfers between devices with their start and end apart: 6, of which 4 were waited for; matrix products, arithmetic and copies ran while one was open for 1% of the time, Pallas kernels for 0%

profile of v1, /device:TPU:7, one launch (start us, length us, event | category | flops | bytes accessed | tf_op | source)
XLA Modules:
  0.0 110.6 jit_solution(10285258323654504818)
XLA Ops:
  0.6 0.0 copy-start
  0.7 0.1 pad_add_fusion.place
  0.7 1.4 %copy-done.1 = bf16[2,1024,256]{2,1,0:T(8,128)(2,1)S(1)} copy-done((bf16[2,1024,256]{2,1,0:T(8,128)(2,1)S(1)}, bf16[2,1024,256]{2,1,0:T(8,128)(2,1)}, u32[]{:S(2)}) %copy-start.1) | copy-done | bytes 1048600
  2.1 1.0 copy-done.3
  3.1 0.9 copy-done.5
  4.1 1.4 %shard_map.76 = (f32[2,32,128]{2,1,0:T(8,128)S(1)}, f32[2,32,128]{2,1,0:T(8,128)S(1)}, f32[3,32,128]{2,1,0:T(8,128)S(1)}, f32[3,32,128]{2,1,0:T(8,128)S(1)}) custom-call(s32[3]{0:T(128)S(1)} %pad_add_fusion.place, bf16[2,1024,256]{2,1,0:T(8,128)(2,1)S(1)} %copy-done.1, bf16[2,128,1024]{2,1,0:T(8,128)(2,1)S(1)} %copy-done.3, f32[160,256]{1,0:T(8,128)S(1)} %bitcast.15), custom_call_target="tpu_custom_call" | custom-call | tf_op jit(solution)/shard_map/pallas_call | solution.py:48
  5.5 3.2 %collective-permute-start = (f32[3,32,128]{2,1,0:T(8,128)S(1)}, f32[3,32,128]{2,1,0:T(8,128)S(1)}, u32[]{:S(2)}, u32[]{:S(2)}) collective-permute-start(f32[3,32,128]{2,1,0:T(8,128)S(1)} %get-tuple-element.12), channel_id=1, source_target_pairs={{0,8},{16,24},{32,40},{48,56},{64,72},{80,88},{96,104},{112,120},{... | collective-permute-start | bytes 147464 | tf_op jit(solution)/shard_map/ppermute | solution.py:189
  8.7 13.6 %collective-permute-start.1 = (f32[3,32,128]{2,1,0:T(8,128)S(1)}, f32[3,32,128]{2,1,0:T(8,128)S(1)}, u32[]{:S(2)}, u32[]{:S(2)}) collective-permute-start(f32[3,32,128]{2,1,0:T(8,128)S(1)} %get-tuple-element.13), channel_id=1, source_target_pairs={{8,16},{24,32},{40,48},{56,64},{72,80},{88,96},{104,112},{120,128}... | collective-permute-start | bytes 147464 | tf_op jit(solution)/shard_map/ppermute | solution.py:188
  22.3 0.0 collective-permute-done
  22.3 2.0 %collective-permute-done.1 = f32[3,32,128]{2,1,0:T(8,128)S(1)} collective-permute-done((f32[3,32,128]{2,1,0:T(8,128)S(1)}, f32[3,32,128]{2,1,0:T(8,128)S(1)}, u32[]{:S(2)}, u32[]{:S(2)}) %collective-permute-start.1) | collective-permute-done | bytes 49184 | tf_op jit(solution)/shard_map/ppermute | solution.py:188
  24.3 13.4 %all-gather = f32[32,32,128]{2,1,0:T(8,128)S(1)} all-gather(f32[8,32,128]{2,1,0:T(8,128)S(1)} %pad_maximum_fusion), channel_id=2, replica_groups={{0,2,4,6},{1,3,5,7},{8,10,12,14},{9,11,13,15},{16,18,20,22},{17,19,21,2..., dimensions={0}, use_global_device_ids=true | all-gather | bytes 655360 | tf_op jit(solution)/shard_map/all_gather | solution.py:208
  37.7 6.1 %collective-permute-start.2 = (f32[4,8,32,128]{3,2,1,0:T(8,128)S(1)}, f32[4,8,32,128]{3,2,1,0:T(8,128)S(1)}, u32[]{:S(2)}, u32[]{:S(2)}) collective-permute-start(f32[4,8,32,128]{3,2,1,0:T(8,128)S(1)} %bitcast.11), channel_id=1, source_target_pairs={{0,1},{1,0},{2,3},{3,2},{4,5},{5,4},{6,7},{7,6},{8,9},{9,8},{10,11... | collective-permute-start | bytes 1572872 | tf_op jit(solution)/shard_map/ppermute | solution.py:209
  43.8 1.5 %collective-permute-done.2.other = f32[4,8,32,128]{3,2,1,0:T(8,128)S(1)} collective-permute-done((f32[4,8,32,128]{3,2,1,0:T(8,128)S(1)}, f32[4,8,32,128]{3,2,1,0:T(8,128)S(1)}, u32[]{:S(2)}, u32[]{:S(2)}) %collective-permute-start.2) | collective-permute-done | bytes 524320 | tf_op jit(solution)/shard_map/ppermute | solution.py:209
  45.3 0.0 copy-done
  45.3 0.0 copy-done.6
  45.3 1.5 %shard_map.77 = f32[4,2,32,128]{3,2,1,0:T(8,128)S(1)} custom-call(s32[3]{0:T(128)S(1)} %pad_add_fusion.place, s32[2,4]{1,0:T(2,128)S(1)} %copy-done.6, f32[4,8,32,128]{3,2,1,0:T(8,128)S(1)} %bitcast.12, f32[4,8,32,128]{3,2,1,0:T(8,128)S(1)} %collective-permute-done.2.other, bf16[2,4,128,1024]{3,2,1,0:T(8,128)(2,1)S(1)} %copy-done), custom_call_target="tpu_custom_call" | custom-call | tf_op jit(solution)/shard_map/pallas_call | solution.py:48
  46.9 0.0 copy-start.2
  46.9 8.8 %all_to_all.10 = f32[4,2,32,128]{3,2,1,0:T(8,128)S(1)} all-to-all(f32[4,2,32,128]{3,2,1,0:T(8,128)S(1)} %shard_map.77), channel_id=1, replica_groups={{0,2,4,6},{1,3,5,7},{8,10,12,14},{9,11,13,15},{16,18,20,22},{17,19,21,2..., dimensions={0} | all-to-all | bytes 262144 | tf_op jit(solution)/shard_map/all_to_all | solution.py:194
  55.7 3.7 %all-gather.1 = f32[8,2,32,128]{3,2,1,0:T(8,128)S(1)} all-gather(f32[4,2,32,128]{3,2,1,0:T(8,128)S(1)} %all_to_all.10), channel_id=3, replica_groups={{0,1},{2,3},{4,5},{6,7},{8,9},{10,11},{12,13},{14,15},{16,17},{18,19},{..., dimensions={0}, use_global_device_ids=true | all-gather | bytes 393216 | tf_op jit(solution)/shard_map/all_gather | solution.py:195
  59.4 0.3 shard_map.78.mine
  59.6 10.4 %collective-permute-start.4 = (f32[2,32,128]{2,1,0:T(8,128)S(1)}, f32[2,32,128]{2,1,0:T(8,128)S(1)}, u32[]{:S(2)}, u32[]{:S(2)}) collective-permute-start(f32[2,32,128]{2,1,0:T(8,128)S(1)} %shard_map.78.mine), channel_id=1, source_target_pairs={{8,16},{24,32},{40,48},{56,64},{72,80},{88,96},{104,112},{120,128}... | collective-permute-start | bytes 98312 | tf_op jit(solution)/shard_map/ppermute | solution.py:188
  70.0 1.9 %collective-permute-start.3 = (f32[2,32,128]{2,1,0:T(8,128)S(1)}, f32[2,32,128]{2,1,0:T(8,128)S(1)}, u32[]{:S(2)}, u32[]{:S(2)}) collective-permute-start(f32[2,32,128]{2,1,0:T(8,128)S(1)} %shard_map.78.mine), channel_id=1, source_target_pairs={{0,8},{16,24},{32,40},{48,56},{64,72},{80,88},{96,104},{112,120},{... | collective-permute-start | bytes 98312 | tf_op jit(solution)/shard_map/ppermute | solution.py:189
  72.0 0.0 collective-permute-done.4
  72.0 2.7 %collective-permute-done.3 = f32[2,32,128]{2,1,0:T(8,128)S(1)} collective-permute-done((f32[2,32,128]{2,1,0:T(8,128)S(1)}, f32[2,32,128]{2,1,0:T(8,128)S(1)}, u32[]{:S(2)}, u32[]{:S(2)}) %collective-permute-start.3) | collective-permute-done | bytes 32800 | tf_op jit(solution)/shard_map/ppermute | solution.py:189
  74.7 17.3 %all-gather.2 = f32[48,32,128]{2,1,0:T(8,128)S(1)} all-gather(f32[6,32,128]{2,1,0:T(8,128)S(1)} %pad_maximum_fusion.1), channel_id=4, replica_groups=mesh['blk'=64,'grp'=8] {'grp'}, dimensions={0}, use_global_device_ids=true | all-gather | bytes 884736 | tf_op jit(solution)/shard_map/all_gather | solution.py:218
  92.0 0.0 copy-done.2
  92.0 6.3 %shard_map.79 = (f32[2,128,32]{2,1,0:T(8,128)S(1)}, f32[4,2,32,128]{3,2,1,0:T(8,128)}, f32[2,32,256]{2,1,0:T(8,128)}) custom-call(s32[3]{0:T(128)S(1)} %pad_add_fusion.place, f32[8,6,32,128]{3,2,1,0:T(8,128)S(1)} %bitcast.10, f32[2,32,128]{2,1,0:T(8,128)S(1)} %shard_map.78.mine, bf16[2,1024,256]{2,1,0:T(8,128)(2,1)S(1)} %copy-done.2, ...), custom_call_target="tpu_custom_call" | custom-call | tf_op jit(solution)/shard_map/pallas_call | solution.py:48
  98.2 3.3 %all-to-all-start.1 = ((f32[4,2,32,128]{3,2,1,0:T(8,128)}), f32[4,2,32,128]{3,2,1,0:T(8,128)S(1)}, u32[]{:S(2)}, u32[]{:S(2)}) async-start(f32[4,2,32,128]{3,2,1,0:T(8,128)} %get-tuple-element.15), calls=%async_computation.1 | async-start | bytes 262144 | tf_op jit(solution)/shard_map/all_to_all | solution.py:194
  101.6 0.7 copy.9
  102.3 4.1 %all-to-all-done.1 = f32[4,2,32,128]{3,2,1,0:T(8,128)S(1)} async-done(((f32[4,2,32,128]{3,2,1,0:T(8,128)}), f32[4,2,32,128]{3,2,1,0:T(8,128)S(1)}, u32[]{:S(2)}, u32[]{:S(2)}) %all-to-all-start.1) | async-done | bytes 131104 | tf_op jit(solution)/shard_map/all_to_all | solution.py:194
  106.4 3.4 %all-gather.3 = f32[8,2,32,128]{3,2,1,0:T(8,128)S(1)} all-gather(f32[4,2,32,128]{3,2,1,0:T(8,128)S(1)} %all-to-all-done.1), channel_id=5, replica_groups={{0,1},{2,3},{4,5},{6,7},{8,9},{10,11},{12,13},{14,15},{16,17},{18,19},{..., dimensions={0}, use_global_device_ids=true | all-gather | bytes 393216 | tf_op jit(solution)/shard_map/all_gather | solution.py:195
  109.8 0.8 shard_map.80
  (8 shorter events, 0.0 us)
Async XLA Ops:
  0.6 44.7 %copy-start = (bf16[2,4,128,1024]{3,2,1,0:T(8,128)(2,1)S(1)}, bf16[2,4,128,1024]{3,2,1,0:T(8,128)(2,1)}, u32[]{:S(2)}) copy-start(bf16[2,4,128,1024]{3,2,1,0:T(8,128)(2,1)} %coup.3) | copy-start | bytes 6291460
  0.7 1.4 %copy-start.1 = (bf16[2,1024,256]{2,1,0:T(8,128)(2,1)S(1)}, bf16[2,1024,256]{2,1,0:T(8,128)(2,1)}, u32[]{:S(2)}) copy-start(bf16[2,1024,256]{2,1,0:T(8,128)(2,1)} %exc.3) | copy-start | bytes 3145732
  2.1 1.0 copy-start.3
  3.1 0.9 copy-start.5
  4.1 41.3 %copy-start.6 = (s32[2,4]{1,0:T(2,128)S(1)}, s32[2,4]{1,0:T(2,128)}, u32[]{:S(2)}) copy-start(s32[2,4]{1,0:T(2,128)} %mask.1) | copy-start | bytes 100
  5.5 16.8 %collective-permute-start = (f32[3,32,128]{2,1,0:T(8,128)S(1)}, f32[3,32,128]{2,1,0:T(8,128)S(1)}, u32[]{:S(2)}, u32[]{:S(2)}) collective-permute-start(f32[3,32,128]{2,1,0:T(8,128)S(1)} %get-tuple-element.12), channel_id=1, source_target_pairs={{0,8},{16,24},{32,40},{48,56},{64,72},{80,88},{96,104},{112,120},{... | collective-permute-start | bytes 147464 | tf_op jit(solution)/shard_map/ppermute | solution.py:189
  8.7 15.6 %collective-permute-start.1 = (f32[3,32,128]{2,1,0:T(8,128)S(1)}, f32[3,32,128]{2,1,0:T(8,128)S(1)}, u32[]{:S(2)}, u32[]{:S(2)}) collective-permute-start(f32[3,32,128]{2,1,0:T(8,128)S(1)} %get-tuple-element.13), channel_id=1, source_target_pairs={{8,16},{24,32},{40,48},{56,64},{72,80},{88,96},{104,112},{120,128}... | collective-permute-start | bytes 147464 | tf_op jit(solution)/shard_map/ppermute | solution.py:188
  37.7 21.7 %copy-start.4 = (bf16[2,128,1024]{2,1,0:T(8,128)(2,1)S(1)}, bf16[2,128,1024]{2,1,0:T(8,128)(2,1)}, u32[]{:S(2)}) copy-start(bf16[2,128,1024]{2,1,0:T(8,128)(2,1)} %inv.3) | copy-start | bytes 1572868
  37.7 7.7 %collective-permute-start.2 = (f32[4,8,32,128]{3,2,1,0:T(8,128)S(1)}, f32[4,8,32,128]{3,2,1,0:T(8,128)S(1)}, u32[]{:S(2)}, u32[]{:S(2)}) collective-permute-start(f32[4,8,32,128]{3,2,1,0:T(8,128)S(1)} %bitcast.11), channel_id=1, source_target_pairs={{0,1},{1,0},{2,3},{3,2},{4,5},{5,4},{6,7},{7,6},{8,9},{9,8},{10,11... | collective-permute-start | bytes 1572872 | tf_op jit(solution)/shard_map/ppermute | solution.py:209
  46.9 45.1 %copy-start.2 = (bf16[2,1024,256]{2,1,0:T(8,128)(2,1)S(1)}, bf16[2,1024,256]{2,1,0:T(8,128)(2,1)}, u32[]{:S(2)}) copy-start(bf16[2,1024,256]{2,1,0:T(8,128)(2,1)} %exc.3) | copy-start | bytes 3145732
  59.6 12.3 %collective-permute-start.4 = (f32[2,32,128]{2,1,0:T(8,128)S(1)}, f32[2,32,128]{2,1,0:T(8,128)S(1)}, u32[]{:S(2)}, u32[]{:S(2)}) collective-permute-start(f32[2,32,128]{2,1,0:T(8,128)S(1)} %shard_map.78.mine), channel_id=1, source_target_pairs={{8,16},{24,32},{40,48},{56,64},{72,80},{88,96},{104,112},{120,128}... | collective-permute-start | bytes 98312 | tf_op jit(solution)/shard_map/ppermute | solution.py:188
  70.0 4.7 %collective-permute-start.3 = (f32[2,32,128]{2,1,0:T(8,128)S(1)}, f32[2,32,128]{2,1,0:T(8,128)S(1)}, u32[]{:S(2)}, u32[]{:S(2)}) collective-permute-start(f32[2,32,128]{2,1,0:T(8,128)S(1)} %shard_map.78.mine), channel_id=1, source_target_pairs={{0,8},{16,24},{32,40},{48,56},{64,72},{80,88},{96,104},{112,120},{... | collective-permute-start | bytes 98312 | tf_op jit(solution)/shard_map/ppermute | solution.py:189
  98.2 8.2 %all-to-all-start.1 = ((f32[4,2,32,128]{3,2,1,0:T(8,128)}), f32[4,2,32,128]{3,2,1,0:T(8,128)S(1)}, u32[]{:S(2)}, u32[]{:S(2)}) async-start(f32[4,2,32,128]{3,2,1,0:T(8,128)} %get-tuple-element.15), calls=%async_computation.1 | async-start | bytes 262144 | tf_op jit(solution)/shard_map/all_to_all | solution.py:194

commit v2 on v1

--- a/solution.py
+++ b/solution.py
@@ -1,5 +1,3 @@
-import functools
-
 import jax
 import jax.numpy as jnp
 from jax import lax
@@ -7,6 +5,7 @@
 from jax.experimental.pallas import tpu as pltpu
 from jax.sharding import PartitionSpec as P
 
+
 F32, BF16 = jnp.float32, jnp.bfloat16
 NT = (((1,), (1,)), ((), ()))
 NN = (((1,), (0,)), ((), ()))
@@ -41,10 +40,11 @@
     return both[:rows] + (both[rows:] + dot(left_high, right_low, dims))
 
 
-def call(kernel, outs, *, scratch=(), smem=0, vmem=32):
+def call(kernel, outs, *, scratch=(), smem=0, hbm=0, vmem=32):
     def run(*args):
         specs = [pl.BlockSpec(memory_space=pltpu.SMEM)] * smem
-        specs += [pl.BlockSpec(memory_space=pltpu.VMEM)] * (len(args) - smem)
+        specs += [pl.BlockSpec(memory_space=pltpu.HBM)] * hbm
+        specs += [pl.BlockSpec(memory_space=pltpu.VMEM)] * (len(args) - smem - hbm)
         return pl.pallas_call(
             kernel,
             out_shape=[jax.ShapeDtypeStruct(shape, F32) for shape in outs],
@@ -57,11 +57,21 @@
     return run
 
 
-def primary_kernel(place, exc, inv, sk, own, local, first, second):
+def primary_kernel(place, exc_hbm, inv_hbm, sk_hbm, own, local, first, second, exc, inv, sk, sems):
+    copies = [pltpu.make_async_copy(sk_hbm, sk, sems.at[0])]
+    for i in range(2):
+        copies.append(pltpu.make_async_copy(inv_hbm.at[i], inv.at[i], sems.at[1 + i]))
+        copies.append(pltpu.make_async_copy(exc_hbm.at[i], exc.at[i], sems.at[3 + i]))
+    for copy in copies:
+        copy.start()
     parity = place[0]
     rows = []
     for i in range(2):
+        copies[1 + 2 * i].wait()
+        copies[2 + 2 * i].wait()
         primary = dot(inv[i], exc[i], NN)
+        if i == 0:
+            copies[0].wait()
         rows.append(exact(sk[...], primary, NT))
         own[i] = rows[i][0:32]
     part = lambda i, k: rows[i][32 * k : 32 * k + 32]
@@ -114,37 +124,68 @@
         out[i] = own[i] - folded(whole, inv[i], NT)
 
 
+def thirds(value):
+    high, rest = value.astype(BF16), value
+    rest = rest - high.astype(F32)
+    middle = rest.astype(BF16)
+    return [high, middle, (rest - middle.astype(F32)).astype(BF16)]
+
+
+def best(left, right, dims):
+    return lax.dot_general(
+        left, right, dims, precision=lax.Precision.HIGHEST, preferred_element_type=F32
+    )
+
+
+def lanes(near, n):
+    return jnp.concatenate([near[g, n] for g in range(8)], axis=1)
+
+
+def products_kernel(place, near, mine, coup, out):
+    even = place[0] == 0
+    own = [lanes(near, 0), lanes(near, 1)]
+    first = [lanes(near, 2), lanes(near, 3)]
+    second = [lanes(near, 4), lanes(near, 5)]
+    before = [jnp.where(even, second[n], first[n]) for n in range(2)]
+    after = [jnp.where(even, first[n], second[n]) for n in range(2)]
+    line = [jnp.concatenate(thirds(w), axis=0) for w in before + own + after]
+    for i in range(2):
+        stack = []
+        for k, o in enumerate((-2, -1, 1, 2)):
+            both = dot(line[2 + i + o], coup[i, k], NT)
+            stack.append(both[:32] + (both[32:64] + both[64:]))
+        value = best(mine[i], jnp.concatenate(stack, axis=0), NT)
+        for z in range(4):
+            out[z, i] = value
+
+
 def lower_inverse(gram):
     n = gram.shape[0]
     row = lax.broadcasted_iota(jnp.int32, (n, 32, 32), 1)
     col = lax.broadcasted_iota(jnp.int32, (n, 32, 32), 2)
-    inverse = jnp.where(row == col, 1.0, 0.0).astype(F32)
-    work = gram
+    work = jnp.concatenate([gram, jnp.where(row == col, 1.0, 0.0).astype(F32)], axis=2)
+    tiles = [work[:, 8 * t : 8 * t + 8] for t in range(4)]
+    within = lax.broadcasted_iota(jnp.int32, (n, 8, 1), 1)
     for j in range(32):
-        scale = lax.rsqrt(work[:, j : j + 1, j : j + 1])
-        pivot = work[:, j : j + 1, :] * scale
-        pivot_inverse = inverse[:, j : j + 1, :] * scale
-        factor = work[:, :, j : j + 1] * scale
-        below = jnp.where(row[:, :, 0:1] > j, factor, 0.0)
-        at = row == j
-        inverse = jnp.where(at, pivot_inverse, inverse - below * pivot_inverse)
-        work = work - below * pivot
-    return inverse
-
-
-def reduce_kernel(place, near, mine, exc, coup, bases, coupled, driven):
-    parity = place[0]
-    whole = []
-    grams = []
-    for n in range(6):
-        w = jnp.concatenate([near[g, n] for g in range(8)], axis=1)
-        whole.append(w)
-        grams.append(
-            lax.dot_general(
-                w, w, NT, precision=lax.Precision.HIGHEST, preferred_element_type=F32
-            )
-            * (1.0 / 1024)
-        )
+        at, r = divmod(j, 8)
+        pivot = tiles[at][:, r : r + 1, :]
+        pivot = pivot * (1.0 / pivot[:, :, j : j + 1])
+        for t in range(at, 4):
+            factor = tiles[t][:, :, j : j + 1]
+            if t == at:
+                factor = jnp.where(within > r, factor, 0.0)
+            tiles[t] = tiles[t] - factor * pivot
+    work = jnp.concatenate(tiles, axis=1)
+    diagonal = jnp.sum(jnp.where(row == col, work[:, :, :32], 0.0), axis=2, keepdims=True)
+    return work[:, :, 32:] * lax.rsqrt(diagonal)
+
+
+def factor_kernel(place, exc_hbm, near, mine, bases, driven, left, right, exc, sem):
+    copy = pltpu.make_async_copy(exc_hbm, exc, sem)
+    copy.start()
+    even = place[0] == 0
+    whole = [lanes(near, n) for n in range(6)]
+    grams = [best(w, w, NT) * (1.0 / 1024) for w in whole]
     diagonal = lax.broadcasted_iota(jnp.int32, (32, 32), 0) == lax.broadcasted_iota(
         jnp.int32, (32, 32), 1
     )
@@ -152,30 +193,33 @@
     grams[4] = grams[4] + absent
     grams[5] = grams[5] + absent
     inverse = lower_inverse(jnp.stack(grams))
-    full = [exact(inverse[n], whole[n], NN) for n in range(6)]
-    even = parity == 0
-    before = [jnp.where(even, full[4 + n], full[2 + n]) for n in range(2)]
-    after = [jnp.where(even, full[2 + n], full[4 + n]) for n in range(2)]
-    line = [before[0], before[1], full[0], full[1], after[0], after[1]]
-    for i in range(2):
-        part = exact(inverse[i], mine[i], NN)
-        bases[i] = part.T
-        driven[i] = folded(full[i], exc[i], NN) * (1.0 / 32)
-        stack = []
+    before = [jnp.where(even, inverse[4 + n], inverse[2 + n]) for n in range(2)]
+    after = [jnp.where(even, inverse[2 + n], inverse[4 + n]) for n in range(2)]
+    line = before + [inverse[0], inverse[1]] + after
+    right[...] = jnp.zeros((2, 128, 128), F32)
+    copy.wait()
+    for i in range(2):
+        bases[i] = exact(inverse[i], mine[i], NN)
+        full = exact(inverse[i], whole[i], NN)
+        driven[i] = folded(full, exc[i], NN) * (1.0 / 32)
+        left[i] = inverse[i] * (1.0 / 32)
         for k, o in enumerate((-2, -1, 1, 2)):
-            stack.append(folded(line[2 + i + o], coup[i, k], NT))
-        value = exact(part, jnp.concatenate(stack, axis=0), NT) * (1.0 / 32)
-        for z in range(4):
-            coupled[z, i] = value
-
-
-def sum_kernel(parts, out):
+            at = slice(32 * k, 32 * k + 32)
+            right[i, at, at] = line[2 + i + o]
+
+
+def sum_kernel(parts, left, right, out):
     total = parts[0, 0]
     for g in range(1, 8):
         total = total + parts[g % 2, g // 2]
     for i in range(2):
+        value = best(best(left[i], total[i], NN), right[i], NT)
         for k in range(4):
-            out[i, k] = total[i, :, 32 * k : 32 * k + 32]
+            out[i, k] = value[:, 32 * k : 32 * k + 32]
+
+
+def in_hbm(value):
+    return pltpu.with_memory_space_constraint(value, pltpu.HBM)
 
 
 def exchange(first, second):
@@ -190,19 +234,31 @@
     return got_first, got_second
 
 
-def share(value):
-    over_chips = lax.all_to_all(value, "grp", 0, 0, axis_index_groups=chip_groups)
-    return lax.all_gather(over_chips, "grp", axis=0, axis_index_groups=core_groups)
+def over_chips(value):
+    return lax.all_to_all(value, "grp", 0, 0, axis_index_groups=chip_groups)
+
+
+def over_cores(value):
+    return lax.all_gather(value, "grp", axis=0, axis_index_groups=core_groups)
 
 
 def shards(excitation, inverse_self, coupling, neighbour_mask, sketch):
-    block_at, member = lax.axis_index("blk"), lax.axis_index("grp")
+    block_at = lax.axis_index("blk")
     inner = (block_at > 0) & (block_at < lax.axis_size("blk") - 1)
-    place = jnp.stack([block_at % 2, member % 2, inner.astype(jnp.int32)])
+    place = jnp.stack([block_at % 2, lax.axis_index("grp") % 2, inner.astype(jnp.int32)])
     turned = sketch.transpose(0, 2, 1).reshape(160, 256)
     own, local, first, second = call(
-        primary_kernel, [(2, 32, 128), (2, 32, 128), (3, 32, 128), (3, 32, 128)], smem=1
-    )(place, excitation, inverse_self, turned)
+        primary_kernel,
+        [(2, 32, 128), (2, 32, 128), (3, 32, 128), (3, 32, 128)],
+        smem=1,
+        hbm=3,
+        scratch=[
+            pltpu.VMEM((2, 1024, 256), BF16),
+            pltpu.VMEM((2, 128, 1024), BF16),
+            pltpu.VMEM((160, 256), F32),
+            pltpu.SemaphoreType.DMA((5,)),
+        ],
+    )(place, in_hbm(excitation), in_hbm(inverse_self), in_hbm(turned))
     got_first, got_second = exchange(first, second)
     pieces = jnp.concatenate([local, got_first, got_second], axis=0)
     same = lax.all_gather(pieces, "grp", axis=0, axis_index_groups=chip_groups)
@@ -213,16 +269,25 @@
         smem=2,
         scratch=[pltpu.VMEM((8, 8, 32, 128), BF16), pltpu.VMEM((8, 8, 32, 128), BF16)],
     )(place, neighbour_mask, same, other, coupling)
-    (sketched,) = call(sketched_kernel, [(2, 32, 128)])(own, share(sources), inverse_self)
+    whole_sources = over_cores(over_chips(sources))
+    (sketched,) = call(sketched_kernel, [(2, 32, 128)])(own, whole_sources, inverse_self)
     got_first, got_second = exchange(sketched, sketched)
     near = lax.all_gather(
         jnp.concatenate([sketched, got_first, got_second], axis=0), "grp", axis=0
     )
-    bases, coupled, driven = call(
-        reduce_kernel, [(2, 128, 32), (4, 2, 32, 128), (2, 32, 256)], smem=1
-    )(place, near, sketched, excitation, coupling)
-    (reduced,) = call(sum_kernel, [(2, 4, 32, 32)])(share(coupled))
-    return bases, reduced, driven
+    (products,) = call(products_kernel, [(4, 2, 32, 128)], smem=1)(
+        place, near, sketched, coupling
+    )
+    parts = over_chips(products)
+    bases, driven, left, right = call(
+        factor_kernel,
+        [(2, 32, 128), (2, 32, 256), (2, 32, 32), (2, 128, 128)],
+        smem=1,
+        hbm=1,
+        scratch=[pltpu.VMEM((2, 1024, 256), BF16), pltpu.SemaphoreType.DMA],
+    )(place, in_hbm(excitation), near, sketched)
+    (reduced,) = call(sum_kernel, [(2, 4, 32, 32)])(over_cores(parts), left, right)
+    return bases.transpose(0, 2, 1), reduced, driven
 
 
 def solution(mesh):

time: 111 us -> 106 us (0.955)
  waiting for transfers between devices: 10.3 us -> 6.2 us
  local copies, waits for them, and re-layouts: 4.02 us -> 0.01 us
  Pallas kernels: 10.3 us -> 13.8 us
    all_to_all x1, waiting for transfers between devices: 4.15 us -> 0.01 us  [over_chips(): return lax.all_to_all(value, 'grp', 0, 0, axis_index_groups=chip_groups)]
    unnamed x15 -> x6, local copies, waits for them, and re-layouts: 4.02 us -> 0.01 us
    pallas_call x5 -> x6, Pallas kernels: 10.3 us -> 13.8 us  [run(): pl.pallas_call(kernel, out_shape=[jax.ShapeDtypeStruct(shape, F32) for sh...]
  transfers between devices with their start and end apart: 6 -> 6, of which waited for: 4 -> 3; matrix products, arithmetic and copies ran while one was open for 1% -> 0% of each run, Pallas kernels for 0% -> 5%
where the time goes in v2:
time: 106 us; the launch traced here: 105 us
  blocking collectives  45.8 us (43%)
  starting transfers between devices  38.5 us (36%)
  Pallas kernels  13.8 us (13%)
  waiting for transfers between devices  6.2 us (6%)
    ppermute x2, starting transfers between devices, exchange(): got_second = lax.ppermute(second, 'blk', pairs(1))  24 us
    all_gather x1, blocking collectives, shards(): lax.all_gather(jnp.concatenate([sketched, got_first, got_second], axis=0)...  17.3 us
    pallas_call x6, Pallas kernels, run(): pl.pallas_call(kernel, out_shape=[jax.ShapeDtypeStruct(shape, F32) for sh...  13.8 us
    all_gather x1, blocking collectives, shards(): same = lax.all_gather(pieces, 'grp', axis=0, axis_index_groups=chip_groups)  13.4 us
    all_to_all x1, blocking collectives, over_chips(): return lax.all_to_all(value, 'grp', 0, 0, axis_index_groups=chip_groups)  8.66 us
    all_gather x2, blocking collectives, over_cores(): return lax.all_gather(value, 'grp', axis=0, axis_index_groups=core_groups)  6.46 us
    ppermute x1, starting transfers between devices, shards(): other = lax.ppermute(same, 'grp', [(g, g ^ 1) for g in range(8)])  6.13 us
    ppermute x2, starting transfers between devices, exchange(): got_first = lax.ppermute(first, 'blk', pairs(0))  5.13 us
  transfers between devices with their start and end apart: 6, of which 3 were waited for; matrix products, arithmetic and copies ran while one was open for 0% of the time, Pallas kernels for 5%

profile of v2, /device:TPU:7, one launch (start us, length us, event | category | flops | bytes accessed | tf_op | source)
XLA Modules:
  0.0 105.2 jit_solution(12327167604902129891)
XLA Ops:
  0.6 0.0 copy-start
  0.6 0.0 copy-start.2
  0.7 0.1 pad_add_fusion.place
  0.8 2.9 %shard_map.76 = (f32[2,32,128]{2,1,0:T(8,128)S(1)}, f32[2,32,128]{2,1,0:T(8,128)S(1)}, f32[3,32,128]{2,1,0:T(8,128)S(1)}, f32[3,32,128]{2,1,0:T(8,128)S(1)}) custom-call(s32[3]{0:T(128)S(1)} %pad_add_fusion.place, bf16[2,1024,256]{2,1,0:T(8,128)(2,1)} %exc_hbm.3, bf16[2,128,1024]{2,1,0:T(8,128)(2,1)} %inv.1, f32[160,256]{1,0:T(8,128)} %bitcast.17), custom_call_target="tpu_custom_call" | custom-call | tf_op jit(solution)/shard_map/pallas_call | solution.py:48
  3.6 3.2 %collective-permute-start = (f32[3,32,128]{2,1,0:T(8,128)S(1)}, f32[3,32,128]{2,1,0:T(8,128)S(1)}, u32[]{:S(2)}, u32[]{:S(2)}) collective-permute-start(f32[3,32,128]{2,1,0:T(8,128)S(1)} %get-tuple-element.13), channel_id=1, source_target_pairs={{0,8},{16,24},{32,40},{48,56},{64,72},{80,88},{96,104},{112,120},{... | collective-permute-start | bytes 147464 | tf_op jit(solution)/shard_map/ppermute | solution.py:233
  6.9 13.6 %collective-permute-start.1 = (f32[3,32,128]{2,1,0:T(8,128)S(1)}, f32[3,32,128]{2,1,0:T(8,128)S(1)}, u32[]{:S(2)}, u32[]{:S(2)}) collective-permute-start(f32[3,32,128]{2,1,0:T(8,128)S(1)} %get-tuple-element.14), channel_id=1, source_target_pairs={{8,16},{24,32},{40,48},{56,64},{72,80},{88,96},{104,112},{120,128}... | collective-permute-start | bytes 147464 | tf_op jit(solution)/shard_map/ppermute | solution.py:232
  20.4 0.0 collective-permute-done
  20.5 2.0 %collective-permute-done.1 = f32[3,32,128]{2,1,0:T(8,128)S(1)} collective-permute-done((f32[3,32,128]{2,1,0:T(8,128)S(1)}, f32[3,32,128]{2,1,0:T(8,128)S(1)}, u32[]{:S(2)}, u32[]{:S(2)}) %collective-permute-start.1) | collective-permute-done | bytes 49184 | tf_op jit(solution)/shard_map/ppermute | solution.py:232
  22.4 13.4 %all-gather = f32[32,32,128]{2,1,0:T(8,128)S(1)} all-gather(f32[8,32,128]{2,1,0:T(8,128)S(1)} %pad_maximum_fusion), channel_id=2, replica_groups={{0,2,4,6},{1,3,5,7},{8,10,12,14},{9,11,13,15},{16,18,20,22},{17,19,21,2..., dimensions={0}, use_global_device_ids=true | all-gather | bytes 655360 | tf_op jit(solution)/shard_map/all_gather | solution.py:264
  35.8 0.0 copy-start.1
  35.8 6.1 %collective-permute-start.2 = (f32[4,8,32,128]{3,2,1,0:T(8,128)S(1)}, f32[4,8,32,128]{3,2,1,0:T(8,128)S(1)}, u32[]{:S(2)}, u32[]{:S(2)}) collective-permute-start(f32[4,8,32,128]{3,2,1,0:T(8,128)S(1)} %bitcast.13), channel_id=1, source_target_pairs={{0,1},{1,0},{2,3},{3,2},{4,5},{5,4},{6,7},{7,6},{8,9},{9,8},{10,11... | collective-permute-start | bytes 1572872 | tf_op jit(solution)/shard_map/ppermute | solution.py:265
  42.0 1.5 %collective-permute-done.2.other = f32[4,8,32,128]{3,2,1,0:T(8,128)S(1)} collective-permute-done((f32[4,8,32,128]{3,2,1,0:T(8,128)S(1)}, f32[4,8,32,128]{3,2,1,0:T(8,128)S(1)}, u32[]{:S(2)}, u32[]{:S(2)}) %collective-permute-start.2) | collective-permute-done | bytes 524320 | tf_op jit(solution)/shard_map/ppermute | solution.py:265
  43.5 0.0 copy-done
  43.5 0.0 copy-done.2
  43.5 1.5 %shard_map.77 = f32[4,2,32,128]{3,2,1,0:T(8,128)S(1)} custom-call(s32[3]{0:T(128)S(1)} %pad_add_fusion.place, s32[2,4]{1,0:T(2,128)S(1)} %copy-done.2, f32[4,8,32,128]{3,2,1,0:T(8,128)S(1)} %bitcast.14, f32[4,8,32,128]{3,2,1,0:T(8,128)S(1)} %collective-permute-done.2.other, bf16[2,4,128,1024]{3,2,1,0:T(8,128)(2,1)S(1)} %copy-done), custom_call_target="tpu_custom_call" | custom-call | tf_op jit(solution)/shard_map/pallas_call | solution.py:48
  45.0 8.7 %all_to_all.10 = f32[4,2,32,128]{3,2,1,0:T(8,128)S(1)} all-to-all(f32[4,2,32,128]{3,2,1,0:T(8,128)S(1)} %shard_map.77), channel_id=1, replica_groups={{0,2,4,6},{1,3,5,7},{8,10,12,14},{9,11,13,15},{16,18,20,22},{17,19,21,2..., dimensions={0} | all-to-all | bytes 262144 | tf_op jit(solution)/shard_map/all_to_all | solution.py:238
  53.7 3.7 %all-gather.1 = f32[8,2,32,128]{3,2,1,0:T(8,128)S(1)} all-gather(f32[4,2,32,128]{3,2,1,0:T(8,128)S(1)} %all_to_all.10), channel_id=3, replica_groups={{0,1},{2,3},{4,5},{6,7},{8,9},{10,11},{12,13},{14,15},{16,17},{18,19},{..., dimensions={0}, use_global_device_ids=true | all-gather | bytes 393216 | tf_op jit(solution)/shard_map/all_gather | solution.py:242
  57.3 0.0 copy-done.1
  57.3 0.3 shard_map.78.mine
  57.6 10.4 %collective-permute-start.4 = (f32[2,32,128]{2,1,0:T(8,128)S(1)}, f32[2,32,128]{2,1,0:T(8,128)S(1)}, u32[]{:S(2)}, u32[]{:S(2)}) collective-permute-start(f32[2,32,128]{2,1,0:T(8,128)S(1)} %shard_map.78.mine), channel_id=1, source_target_pairs={{8,16},{24,32},{40,48},{56,64},{72,80},{88,96},{104,112},{120,128}... | collective-permute-start | bytes 98312 | tf_op jit(solution)/shard_map/ppermute | solution.py:232
  68.0 1.9 %collective-permute-start.3 = (f32[2,32,128]{2,1,0:T(8,128)S(1)}, f32[2,32,128]{2,1,0:T(8,128)S(1)}, u32[]{:S(2)}, u32[]{:S(2)}) collective-permute-start(f32[2,32,128]{2,1,0:T(8,128)S(1)} %shard_map.78.mine), channel_id=1, source_target_pairs={{0,8},{16,24},{32,40},{48,56},{64,72},{80,88},{96,104},{112,120},{... | collective-permute-start | bytes 98312 | tf_op jit(solution)/shard_map/ppermute | solution.py:233
  70.0 0.0 collective-permute-done.4
  70.0 2.7 %collective-permute-done.3 = f32[2,32,128]{2,1,0:T(8,128)S(1)} collective-permute-done((f32[2,32,128]{2,1,0:T(8,128)S(1)}, f32[2,32,128]{2,1,0:T(8,128)S(1)}, u32[]{:S(2)}, u32[]{:S(2)}) %collective-permute-start.3) | collective-permute-done | bytes 32800 | tf_op jit(solution)/shard_map/ppermute | solution.py:233
  72.7 17.3 %all-gather.2 = f32[48,32,128]{2,1,0:T(8,128)S(1)} all-gather(f32[6,32,128]{2,1,0:T(8,128)S(1)} %pad_maximum_fusion.1), channel_id=4, replica_groups=mesh['blk'=64,'grp'=8] {'grp'}, dimensions={0}, use_global_device_ids=true | all-gather | bytes 884736 | tf_op jit(solution)/shard_map/all_gather | solution.py:275
  90.0 2.5 %shard_map.80 = f32[4,2,32,128]{3,2,1,0:T(8,128)} custom-call(s32[3]{0:T(128)S(1)} %pad_add_fusion.place, f32[8,6,32,128]{3,2,1,0:T(8,128)S(1)} %bitcast.11, f32[2,32,128]{2,1,0:T(8,128)S(1)} %shard_map.78.mine, bf16[2,4,128,1024]{3,2,1,0:T(8,128)(2,1)S(1)} %copy-done), custom_call_target="tpu_custom_call" | custom-call | tf_op jit(solution)/shard_map/pallas_call | solution.py:48
  92.4 3.3 %all-to-all-start.1 = ((f32[4,2,32,128]{3,2,1,0:T(8,128)}), f32[4,2,32,128]{3,2,1,0:T(8,128)S(1)}, u32[]{:S(2)}, u32[]{:S(2)}) async-start(f32[4,2,32,128]{3,2,1,0:T(8,128)} %shard_map.80), calls=%async_computation.1 | async-start | bytes 262144 | tf_op jit(solution)/shard_map/all_to_all | solution.py:238
  95.8 5.5 %shard_map.79 = (f32[2,32,128]{2,1,0:T(8,128)}, f32[2,32,256]{2,1,0:T(8,128)}, f32[2,32,32]{2,1,0:T(8,128)S(1)}, f32[2,128,128]{2,1,0:T(8,128)S(1)}) custom-call(s32[3]{0:T(128)S(1)} %pad_add_fusion.place, bf16[2,1024,256]{2,1,0:T(8,128)(2,1)} %exc_hbm.3, f32[8,6,32,128]{3,2,1,0:T(8,128)S(1)} %bitcast.12, f32[2,32,128]{2,1,0:T(8,128)S(1)} %shard_map.78.mine), custom_call_target="tpu_custom_call" | custom-call | tf_op jit(solution)/shard_map/pallas_call | solution.py:48
  101.2 0.0 all-to-all-done.1
  101.2 2.8 %all-gather.3 = f32[8,2,32,128]{3,2,1,0:T(8,128)S(1)} all-gather(f32[4,2,32,128]{3,2,1,0:T(8,128)S(1)} %all-to-all-done.1), channel_id=5, replica_groups={{0,1},{2,3},{4,5},{6,7},{8,9},{10,11},{12,13},{14,15},{16,17},{18,19},{..., dimensions={0}, use_global_device_ids=true | all-gather | bytes 393216 | tf_op jit(solution)/shard_map/all_gather | solution.py:242
  104.0 1.2 %shard_map.81 = f32[2,4,32,32]{3,2,1,0:T(8,128)} custom-call(f32[2,4,2,32,128]{4,3,2,1,0:T(8,128)S(1)} %bitcast.16, f32[2,32,32]{2,1,0:T(8,128)S(1)} %get-tuple-element.16.left, f32[2,128,128]{2,1,0:T(8,128)S(1)} %get-tuple-element.17.right), custom_call_target="tpu_custom_call" | custom-call | tf_op jit(solution)/shard_map/pallas_call | solution.py:48
  (2 shorter events, 0.0 us)
Async XLA Ops:
  0.6 42.8 %copy-start = (bf16[2,4,128,1024]{3,2,1,0:T(8,128)(2,1)S(1)}, bf16[2,4,128,1024]{3,2,1,0:T(8,128)(2,1)}, u32[]{:S(2)}) copy-start(bf16[2,4,128,1024]{3,2,1,0:T(8,128)(2,1)} %coup.3) | copy-start | bytes 6291460
  0.6 42.8 %copy-start.2 = (s32[2,4]{1,0:T(2,128)S(1)}, s32[2,4]{1,0:T(2,128)}, u32[]{:S(2)}) copy-start(s32[2,4]{1,0:T(2,128)} %mask.1) | copy-start | bytes 100
  3.6 16.8 %collective-permute-start = (f32[3,32,128]{2,1,0:T(8,128)S(1)}, f32[3,32,128]{2,1,0:T(8,128)S(1)}, u32[]{:S(2)}, u32[]{:S(2)}) collective-permute-start(f32[3,32,128]{2,1,0:T(8,128)S(1)} %get-tuple-element.13), channel_id=1, source_target_pairs={{0,8},{16,24},{32,40},{48,56},{64,72},{80,88},{96,104},{112,120},{... | collective-permute-start | bytes 147464 | tf_op jit(solution)/shard_map/ppermute | solution.py:233
  6.9 15.6 %collective-permute-start.1 = (f32[3,32,128]{2,1,0:T(8,128)S(1)}, f32[3,32,128]{2,1,0:T(8,128)S(1)}, u32[]{:S(2)}, u32[]{:S(2)}) collective-permute-start(f32[3,32,128]{2,1,0:T(8,128)S(1)} %get-tuple-element.14), channel_id=1, source_target_pairs={{8,16},{24,32},{40,48},{56,64},{72,80},{88,96},{104,112},{120,128}... | collective-permute-start | bytes 147464 | tf_op jit(solution)/shard_map/ppermute | solution.py:232
  35.8 21.5 %copy-start.1 = (bf16[2,128,1024]{2,1,0:T(8,128)(2,1)S(1)}, bf16[2,128,1024]{2,1,0:T(8,128)(2,1)}, u32[]{:S(2)}) copy-start(bf16[2,128,1024]{2,1,0:T(8,128)(2,1)} %inv.1) | copy-start | bytes 1572868
  35.8 7.7 %collective-permute-start.2 = (f32[4,8,32,128]{3,2,1,0:T(8,128)S(1)}, f32[4,8,32,128]{3,2,1,0:T(8,128)S(1)}, u32[]{:S(2)}, u32[]{:S(2)}) collective-permute-start(f32[4,8,32,128]{3,2,1,0:T(8,128)S(1)} %bitcast.13), channel_id=1, source_target_pairs={{0,1},{1,0},{2,3},{3,2},{4,5},{5,4},{6,7},{7,6},{8,9},{9,8},{10,11... | collective-permute-start | bytes 1572872 | tf_op jit(solution)/shard_map/ppermute | solution.py:265
  57.6 12.3 %collective-permute-start.4 = (f32[2,32,128]{2,1,0:T(8,128)S(1)}, f32[2,32,128]{2,1,0:T(8,128)S(1)}, u32[]{:S(2)}, u32[]{:S(2)}) collective-permute-start(f32[2,32,128]{2,1,0:T(8,128)S(1)} %shard_map.78.mine), channel_id=1, source_target_pairs={{8,16},{24,32},{40,48},{56,64},{72,80},{88,96},{104,112},{120,128}... | collective-permute-start | bytes 98312 | tf_op jit(solution)/shard_map/ppermute | solution.py:232
  68.0 4.7 %collective-permute-start.3 = (f32[2,32,128]{2,1,0:T(8,128)S(1)}, f32[2,32,128]{2,1,0:T(8,128)S(1)}, u32[]{:S(2)}, u32[]{:S(2)}) collective-permute-start(f32[2,32,128]{2,1,0:T(8,128)S(1)} %shard_map.78.mine), channel_id=1, source_target_pairs={{0,8},{16,24},{32,40},{48,56},{64,72},{80,88},{96,104},{112,120},{... | collective-permute-start | bytes 98312 | tf_op jit(solution)/shard_map/ppermute | solution.py:233
  92.4 8.8 %all-to-all-start.1 = ((f32[4,2,32,128]{3,2,1,0:T(8,128)}), f32[4,2,32,128]{3,2,1,0:T(8,128)S(1)}, u32[]{:S(2)}, u32[]{:S(2)}) async-start(f32[4,2,32,128]{3,2,1,0:T(8,128)} %shard_map.80), calls=%async_computation.1 | async-start | bytes 262144 | tf_op jit(solution)/shard_map/all_to_all | solution.py:238

commit v3 on v2

--- a/solution.py
+++ b/solution.py
@@ -11,6 +11,7 @@
 NN = (((1,), (0,)), ((), ()))
 chip_groups = [[0, 2, 4, 6], [1, 3, 5, 7]]
 core_groups = [[0, 1], [2, 3], [4, 5], [6, 7]]
+run_length = 8
 
 
 def halves(value):
@@ -86,13 +87,14 @@
 
 
 def sources_kernel(place, mask, same, other, coup, out, high, low):
-    parity, core = place[0], place[1]
+    parity, core, turn = place[0], place[1], place[3]
     for z in range(4):
         for piece in range(8):
             for src, c in ((same, core), (other, 1 - core)):
-                h, l = halves(src[z, piece])
-                high[2 * z + c, piece] = h
-                low[2 * z + c, piece] = l
+                g = 2 * z + c
+                if piece >= 5:
+                    g = (g + 4 * turn) & 7
+                high[g, piece], low[g, piece] = halves(src[z, piece])
 
     def piece_of(n):
         return jnp.concatenate(
@@ -137,15 +139,16 @@
     )
 
 
-def lanes(near, n):
-    return jnp.concatenate([near[g, n] for g in range(8)], axis=1)
+def lanes(near, n, turn=None):
+    at = range(8) if turn is None else [(g + 4 * turn) & 7 for g in range(8)]
+    return jnp.concatenate([near[g, n] for g in at], axis=1)
 
 
 def products_kernel(place, near, mine, coup, out):
     even = place[0] == 0
     own = [lanes(near, 0), lanes(near, 1)]
     first = [lanes(near, 2), lanes(near, 3)]
-    second = [lanes(near, 4), lanes(near, 5)]
+    second = [lanes(near, 4, place[3]), lanes(near, 5, place[3])]
     before = [jnp.where(even, second[n], first[n]) for n in range(2)]
     after = [jnp.where(even, first[n], second[n]) for n in range(2)]
     line = [jnp.concatenate(thirds(w), axis=0) for w in before + own + after]
@@ -185,7 +188,7 @@
     copy.start()
     even = place[0] == 0
     whole = [lanes(near, n) for n in range(6)]
-    grams = [best(w, w, NT) * (1.0 / 1024) for w in whole]
+    grams = [exact(w, w, NT) * (1.0 / 1024) for w in whole]
     diagonal = lax.broadcasted_iota(jnp.int32, (32, 32), 0) == lax.broadcasted_iota(
         jnp.int32, (32, 32), 1
     )
@@ -222,15 +225,25 @@
     return pltpu.with_memory_space_constraint(value, pltpu.HBM)
 
 
+def in_vmem(value):
+    return pltpu.with_memory_space_constraint(value, pltpu.VMEM)
+
+
 def exchange(first, second):
-    size = lax.axis_size("blk")
+    size, width = lax.axis_size("blk"), lax.axis_size("grp")
 
     def pairs(start):
-        ups = [(i, i + 1) for i in range(start, size - 1, 2)]
-        return ups + [(j, i) for i, j in ups]
-
-    got_second = lax.ppermute(second, "blk", pairs(1))
-    got_first = lax.ppermute(first, "blk", pairs(0))
+        both = []
+        for i in range(start, size - 1, 2):
+            turn = width // 2 if i % run_length == run_length - 1 else 0
+            for g in range(width):
+                here, there = i * width + g, (i + 1) * width + (g ^ turn)
+                both += [(here, there), (there, here)]
+        return both
+
+    axes = ("blk", "grp")
+    got_second = lax.ppermute(second, axes, pairs(1))
+    got_first = lax.ppermute(first, axes, pairs(0))
     return got_first, got_second
 
 
@@ -245,8 +258,11 @@
 def shards(excitation, inverse_self, coupling, neighbour_mask, sketch):
     block_at = lax.axis_index("blk")
     inner = (block_at > 0) & (block_at < lax.axis_size("blk") - 1)
-    place = jnp.stack([block_at % 2, lax.axis_index("grp") % 2, inner.astype(jnp.int32)])
-    turned = sketch.transpose(0, 2, 1).reshape(160, 256)
+    turned = ((block_at + 1) % run_length) < 2
+    place = jnp.stack(
+        [block_at % 2, lax.axis_index("grp") % 2, inner.astype(jnp.int32), turned.astype(jnp.int32)]
+    )
+    tests = sketch.transpose(0, 2, 1).reshape(160, 256)
     own, local, first, second = call(
         primary_kernel,
         [(2, 32, 128), (2, 32, 128), (3, 32, 128), (3, 32, 128)],
@@ -258,7 +274,7 @@
             pltpu.VMEM((160, 256), F32),
             pltpu.SemaphoreType.DMA((5,)),
         ],
-    )(place, in_hbm(excitation), in_hbm(inverse_self), in_hbm(turned))
+    )(place, in_hbm(excitation), in_hbm(inverse_self), in_hbm(tests))
     got_first, got_second = exchange(first, second)
     pieces = jnp.concatenate([local, got_first, got_second], axis=0)
     same = lax.all_gather(pieces, "grp", axis=0, axis_index_groups=chip_groups)
@@ -278,7 +294,7 @@
     (products,) = call(products_kernel, [(4, 2, 32, 128)], smem=1)(
         place, near, sketched, coupling
     )
-    parts = over_chips(products)
+    parts = over_chips(in_vmem(products))
     bases, driven, left, right = call(
         factor_kernel,
         [(2, 32, 128), (2, 32, 256), (2, 32, 32), (2, 128, 128)],
@@ -286,7 +302,7 @@
         hbm=1,
         scratch=[pltpu.VMEM((2, 1024, 256), BF16), pltpu.SemaphoreType.DMA],
     )(place, in_hbm(excitation), near, sketched)
-    (reduced,) = call(sum_kernel, [(2, 4, 32, 32)])(over_cores(parts), left, right)
+    (reduced,) = call(sum_kernel, [(2, 4, 32, 32)])(over_cores(parts), in_vmem(left), in_vmem(right))
     return bases.transpose(0, 2, 1), reduced, driven
 
 

time: 106 us -> 103 us (0.972)
  starting transfers between devices: 38.5 us -> 37 us
  blocking collectives: 45.8 us -> 44.6 us
    ppermute x4, starting transfers between devices: 29.1 us -> 26.8 us  [the longest x2 21.6 us: exchange(): got_second = lax.ppermute(second, axes, pairs(1))]
    all_to_all x1, blocking collectives: 8.66 us -> 7.26 us  [over_chips(): return lax.all_to_all(value, 'grp', 0, 0, axis_index_groups=chip_groups)]
where the time goes in v3:
time: 103 us; the launch traced here: 102 us
  blocking collectives  44.6 us (43%)
  starting transfers between devices  37 us (36%)
  Pallas kernels  13.5 us (13%)
  waiting for transfers between devices  6.21 us (6%)
    ppermute x2, starting transfers between devices, exchange(): got_second = lax.ppermute(second, axes, pairs(1))  21.6 us
    all_gather x1, blocking collectives, shards(): lax.all_gather(jnp.concatenate([sketched, got_first, got_second], axis=0)...  17.3 us
    pallas_call x6, Pallas kernels, run(): pl.pallas_call(kernel, out_shape=[jax.ShapeDtypeStruct(shape, F32) for sh...  13.5 us
    all_gather x1, blocking collectives, shards(): same = lax.all_gather(pieces, 'grp', axis=0, axis_index_groups=chip_groups)  13.2 us
    all_to_all x1, blocking collectives, over_chips(): return lax.all_to_all(value, 'grp', 0, 0, axis_index_groups=chip_groups)  7.26 us
    all_gather x2, blocking collectives, over_cores(): return lax.all_gather(value, 'grp', axis=0, axis_index_groups=core_groups)  6.85 us
    ppermute x1, starting transfers between devices, shards(): other = lax.ppermute(same, 'grp', [(g, g ^ 1) for g in range(8)])  6.49 us
    ppermute x2, starting transfers between devices, exchange(): got_first = lax.ppermute(first, axes, pairs(0))  5.12 us
  transfers between devices with their start and end apart: 6, of which 3 were waited for; matrix products, arithmetic and copies ran while one was open for 0% of the time, Pallas kernels for 5%

profile of v3, /device:TPU:7, one launch (start us, length us, event | category | flops | bytes accessed | tf_op | source)
XLA Modules:
  0.0 102.2 jit_solution(560474152490182186)
XLA Ops:
  0.6 0.0 copy-start
  0.6 0.0 copy-start.2
  0.7 0.1 pad_add_fusion.place
  0.8 2.9 %shard_map.76 = (f32[2,32,128]{2,1,0:T(8,128)S(1)}, f32[2,32,128]{2,1,0:T(8,128)S(1)}, f32[3,32,128]{2,1,0:T(8,128)S(1)}, f32[3,32,128]{2,1,0:T(8,128)S(1)}) custom-call(s32[4]{0:T(128)S(1)} %pad_add_fusion.place, bf16[2,1024,256]{2,1,0:T(8,128)(2,1)} %exc_hbm.3, bf16[2,128,1024]{2,1,0:T(8,128)(2,1)} %inv.1, f32[160,256]{1,0:T(8,128)} %bitcast.18), custom_call_target="tpu_custom_call" | custom-call | tf_op jit(solution)/shard_map/pallas_call | solution.py:49
  3.7 3.2 %collective-permute-start = (f32[3,32,128]{2,1,0:T(8,128)S(1)}, f32[3,32,128]{2,1,0:T(8,128)S(1)}, u32[]{:S(2)}, u32[]{:S(2)}) collective-permute-start(f32[3,32,128]{2,1,0:T(8,128)S(1)} %get-tuple-element.13), channel_id=1, source_target_pairs={{0,8},{8,0},{1,9},{9,1},{2,10},{10,2},{3,11},{11,3},{4,12},{12,4},... | collective-permute-start | bytes 147464 | tf_op jit(solution)/shard_map/ppermute | solution.py:246
  6.9 13.6 %collective-permute-start.1 = (f32[3,32,128]{2,1,0:T(8,128)S(1)}, f32[3,32,128]{2,1,0:T(8,128)S(1)}, u32[]{:S(2)}, u32[]{:S(2)}) collective-permute-start(f32[3,32,128]{2,1,0:T(8,128)S(1)} %get-tuple-element.14), channel_id=1, source_target_pairs={{8,16},{16,8},{9,17},{17,9},{10,18},{18,10},{11,19},{19,11},{12,20... | collective-permute-start | bytes 147464 | tf_op jit(solution)/shard_map/ppermute | solution.py:245
  20.5 0.0 collective-permute-done
  20.5 2.0 %collective-permute-done.1 = f32[3,32,128]{2,1,0:T(8,128)S(1)} collective-permute-done((f32[3,32,128]{2,1,0:T(8,128)S(1)}, f32[3,32,128]{2,1,0:T(8,128)S(1)}, u32[]{:S(2)}, u32[]{:S(2)}) %collective-permute-start.1) | collective-permute-done | bytes 49184 | tf_op jit(solution)/shard_map/ppermute | solution.py:245
  22.5 13.2 %all-gather = f32[32,32,128]{2,1,0:T(8,128)S(1)} all-gather(f32[8,32,128]{2,1,0:T(8,128)S(1)} %pad_maximum_fusion), channel_id=2, replica_groups={{0,2,4,6},{1,3,5,7},{8,10,12,14},{9,11,13,15},{16,18,20,22},{17,19,21,2..., dimensions={0}, use_global_device_ids=true | all-gather | bytes 655360 | tf_op jit(solution)/shard_map/all_gather | solution.py:280
  35.7 0.0 copy-start.1
  35.7 6.5 %collective-permute-start.2 = (f32[4,8,32,128]{3,2,1,0:T(8,128)S(1)}, f32[4,8,32,128]{3,2,1,0:T(8,128)S(1)}, u32[]{:S(2)}, u32[]{:S(2)}) collective-permute-start(f32[4,8,32,128]{3,2,1,0:T(8,128)S(1)} %bitcast.14), channel_id=1, source_target_pairs={{0,1},{1,0},{2,3},{3,2},{4,5},{5,4},{6,7},{7,6},{8,9},{9,8},{10,11... | collective-permute-start | bytes 1572872 | tf_op jit(solution)/shard_map/ppermute | solution.py:281
  42.2 1.5 %collective-permute-done.2.other = f32[4,8,32,128]{3,2,1,0:T(8,128)S(1)} collective-permute-done((f32[4,8,32,128]{3,2,1,0:T(8,128)S(1)}, f32[4,8,32,128]{3,2,1,0:T(8,128)S(1)}, u32[]{:S(2)}, u32[]{:S(2)}) %collective-permute-start.2) | collective-permute-done | bytes 524320 | tf_op jit(solution)/shard_map/ppermute | solution.py:281
  43.7 0.0 copy-done
  43.7 0.0 copy-done.2
  43.7 1.5 %shard_map.77 = f32[4,2,32,128]{3,2,1,0:T(8,128)S(1)} custom-call(s32[4]{0:T(128)S(1)} %pad_add_fusion.place, s32[2,4]{1,0:T(2,128)S(1)} %copy-done.2, f32[4,8,32,128]{3,2,1,0:T(8,128)S(1)} %bitcast.15, f32[4,8,32,128]{3,2,1,0:T(8,128)S(1)} %collective-permute-done.2.other, bf16[2,4,128,1024]{3,2,1,0:T(8,128)(2,1)S(1)} %copy-done), custom_call_target="tpu_custom_call" | custom-call | tf_op jit(solution)/shard_map/pallas_call | solution.py:49
  45.2 7.3 %all_to_all.10 = f32[4,2,32,128]{3,2,1,0:T(8,128)S(1)} all-to-all(f32[4,2,32,128]{3,2,1,0:T(8,128)S(1)} %shard_map.77), channel_id=1, replica_groups={{0,2,4,6},{1,3,5,7},{8,10,12,14},{9,11,13,15},{16,18,20,22},{17,19,21,2..., dimensions={0} | all-to-all | bytes 262144 | tf_op jit(solution)/shard_map/all_to_all | solution.py:251
  52.5 3.5 %all-gather.1 = f32[8,2,32,128]{3,2,1,0:T(8,128)S(1)} all-gather(f32[4,2,32,128]{3,2,1,0:T(8,128)S(1)} %all_to_all.10), channel_id=3, replica_groups={{0,1},{2,3},{4,5},{6,7},{8,9},{10,11},{12,13},{14,15},{16,17},{18,19},{..., dimensions={0}, use_global_device_ids=true | all-gather | bytes 393216 | tf_op jit(solution)/shard_map/all_gather | solution.py:255
  56.0 0.0 copy-done.1
  56.0 0.3 shard_map.78.mine
  56.3 8.0 %collective-permute-start.4 = (f32[2,32,128]{2,1,0:T(8,128)S(1)}, f32[2,32,128]{2,1,0:T(8,128)S(1)}, u32[]{:S(2)}, u32[]{:S(2)}) collective-permute-start(f32[2,32,128]{2,1,0:T(8,128)S(1)} %shard_map.78.mine), channel_id=1, source_target_pairs={{8,16},{16,8},{9,17},{17,9},{10,18},{18,10},{11,19},{19,11},{12,20... | collective-permute-start | bytes 98312 | tf_op jit(solution)/shard_map/ppermute | solution.py:245
  64.4 1.9 %collective-permute-start.3 = (f32[2,32,128]{2,1,0:T(8,128)S(1)}, f32[2,32,128]{2,1,0:T(8,128)S(1)}, u32[]{:S(2)}, u32[]{:S(2)}) collective-permute-start(f32[2,32,128]{2,1,0:T(8,128)S(1)} %shard_map.78.mine), channel_id=1, source_target_pairs={{0,8},{8,0},{1,9},{9,1},{2,10},{10,2},{3,11},{11,3},{4,12},{12,4},... | collective-permute-start | bytes 98312 | tf_op jit(solution)/shard_map/ppermute | solution.py:246
  66.3 0.0 collective-permute-done.4
  66.3 2.7 %collective-permute-done.3 = f32[2,32,128]{2,1,0:T(8,128)S(1)} collective-permute-done((f32[2,32,128]{2,1,0:T(8,128)S(1)}, f32[2,32,128]{2,1,0:T(8,128)S(1)}, u32[]{:S(2)}, u32[]{:S(2)}) %collective-permute-start.3) | collective-permute-done | bytes 32800 | tf_op jit(solution)/shard_map/ppermute | solution.py:246
  69.1 17.3 %all-gather.2 = f32[48,32,128]{2,1,0:T(8,128)S(1)} all-gather(f32[6,32,128]{2,1,0:T(8,128)S(1)} %pad_maximum_fusion.1), channel_id=4, replica_groups=mesh['blk'=64,'grp'=8] {'grp'}, dimensions={0}, use_global_device_ids=true | all-gather | bytes 884736 | tf_op jit(solution)/shard_map/all_gather | solution.py:291
  86.3 2.5 %shard_map.80 = f32[4,2,32,128]{3,2,1,0:T(8,128)} custom-call(s32[4]{0:T(128)S(1)} %pad_add_fusion.place, f32[8,6,32,128]{3,2,1,0:T(8,128)S(1)} %bitcast.12, f32[2,32,128]{2,1,0:T(8,128)S(1)} %shard_map.78.mine, bf16[2,4,128,1024]{3,2,1,0:T(8,128)(2,1)S(1)} %copy-done), custom_call_target="tpu_custom_call" | custom-call | tf_op jit(solution)/shard_map/pallas_call | solution.py:49
  88.8 3.7 %all-to-all-start.1 = ((f32[4,2,32,128]{3,2,1,0:T(8,128)}), f32[4,2,32,128]{3,2,1,0:T(8,128)S(1)}, u32[]{:S(2)}, u32[]{:S(2)}) async-start(f32[4,2,32,128]{3,2,1,0:T(8,128)} %shard_map.80), calls=%async_computation.1 | async-start | bytes 262144 | tf_op jit(solution)/shard_map/all_to_all | solution.py:251
  92.5 5.2 %shard_map.79 = (f32[2,32,128]{2,1,0:T(8,128)}, f32[2,32,256]{2,1,0:T(8,128)}, f32[2,32,32]{2,1,0:T(8,128)S(1)}, f32[2,128,128]{2,1,0:T(8,128)S(1)}) custom-call(s32[4]{0:T(128)S(1)} %pad_add_fusion.place, bf16[2,1024,256]{2,1,0:T(8,128)(2,1)} %exc_hbm.3, f32[8,6,32,128]{3,2,1,0:T(8,128)S(1)} %bitcast.13, f32[2,32,128]{2,1,0:T(8,128)S(1)} %shard_map.78.mine), custom_call_target="tpu_custom_call" | custom-call | tf_op jit(solution)/shard_map/pallas_call | solution.py:49
  97.7 0.0 all-to-all-done.1
  97.7 3.3 %all-gather.3 = f32[8,2,32,128]{3,2,1,0:T(8,128)S(1)} all-gather(f32[4,2,32,128]{3,2,1,0:T(8,128)S(1)} %all-to-all-done.1), channel_id=5, replica_groups={{0,1},{2,3},{4,5},{6,7},{8,9},{10,11},{12,13},{14,15},{16,17},{18,19},{..., dimensions={0}, use_global_device_ids=true | all-gather | bytes 393216 | tf_op jit(solution)/shard_map/all_gather | solution.py:255
  101.0 1.2 %shard_map.81 = f32[2,4,32,32]{3,2,1,0:T(8,128)} custom-call(f32[2,4,2,32,128]{4,3,2,1,0:T(8,128)S(1)} %bitcast.17, f32[2,32,32]{2,1,0:T(8,128)S(1)} %get-tuple-element.16.left, f32[2,128,128]{2,1,0:T(8,128)S(1)} %get-tuple-element.17.right), custom_call_target="tpu_custom_call" | custom-call | tf_op jit(solution)/shard_map/pallas_call | solution.py:49
  (2 shorter events, 0.0 us)
Async XLA Ops:
  0.6 43.1 %copy-start = (bf16[2,4,128,1024]{3,2,1,0:T(8,128)(2,1)S(1)}, bf16[2,4,128,1024]{3,2,1,0:T(8,128)(2,1)}, u32[]{:S(2)}) copy-start(bf16[2,4,128,1024]{3,2,1,0:T(8,128)(2,1)} %coup.3) | copy-start | bytes 6291460
  0.6 43.1 %copy-start.2 = (s32[2,4]{1,0:T(2,128)S(1)}, s32[2,4]{1,0:T(2,128)}, u32[]{:S(2)}) copy-start(s32[2,4]{1,0:T(2,128)} %mask.1) | copy-start | bytes 100
  3.7 16.8 %collective-permute-start = (f32[3,32,128]{2,1,0:T(8,128)S(1)}, f32[3,32,128]{2,1,0:T(8,128)S(1)}, u32[]{:S(2)}, u32[]{:S(2)}) collective-permute-start(f32[3,32,128]{2,1,0:T(8,128)S(1)} %get-tuple-element.13), channel_id=1, source_target_pairs={{0,8},{8,0},{1,9},{9,1},{2,10},{10,2},{3,11},{11,3},{4,12},{12,4},... | collective-permute-start | bytes 147464 | tf_op jit(solution)/shard_map/ppermute | solution.py:246
  6.9 15.6 %collective-permute-start.1 = (f32[3,32,128]{2,1,0:T(8,128)S(1)}, f32[3,32,128]{2,1,0:T(8,128)S(1)}, u32[]{:S(2)}, u32[]{:S(2)}) collective-permute-start(f32[3,32,128]{2,1,0:T(8,128)S(1)} %get-tuple-element.14), channel_id=1, source_target_pairs={{8,16},{16,8},{9,17},{17,9},{10,18},{18,10},{11,19},{19,11},{12,20... | collective-permute-start | bytes 147464 | tf_op jit(solution)/shard_map/ppermute | solution.py:245
  35.7 20.3 %copy-start.1 = (bf16[2,128,1024]{2,1,0:T(8,128)(2,1)S(1)}, bf16[2,128,1024]{2,1,0:T(8,128)(2,1)}, u32[]{:S(2)}) copy-start(bf16[2,128,1024]{2,1,0:T(8,128)(2,1)} %inv.1) | copy-start | bytes 1572868
  35.7 8.0 %collective-permute-start.2 = (f32[4,8,32,128]{3,2,1,0:T(8,128)S(1)}, f32[4,8,32,128]{3,2,1,0:T(8,128)S(1)}, u32[]{:S(2)}, u32[]{:S(2)}) collective-permute-start(f32[4,8,32,128]{3,2,1,0:T(8,128)S(1)} %bitcast.14), channel_id=1, source_target_pairs={{0,1},{1,0},{2,3},{3,2},{4,5},{5,4},{6,7},{7,6},{8,9},{9,8},{10,11... | collective-permute-start | bytes 1572872 | tf_op jit(solution)/shard_map/ppermute | solution.py:281
  56.3 10.0 %collective-permute-start.4 = (f32[2,32,128]{2,1,0:T(8,128)S(1)}, f32[2,32,128]{2,1,0:T(8,128)S(1)}, u32[]{:S(2)}, u32[]{:S(2)}) collective-permute-start(f32[2,32,128]{2,1,0:T(8,128)S(1)} %shard_map.78.mine), channel_id=1, source_target_pairs={{8,16},{16,8},{9,17},{17,9},{10,18},{18,10},{11,19},{19,11},{12,20... | collective-permute-start | bytes 98312 | tf_op jit(solution)/shard_map/ppermute | solution.py:245
  64.4 4.7 %collective-permute-start.3 = (f32[2,32,128]{2,1,0:T(8,128)S(1)}, f32[2,32,128]{2,1,0:T(8,128)S(1)}, u32[]{:S(2)}, u32[]{:S(2)}) collective-permute-start(f32[2,32,128]{2,1,0:T(8,128)S(1)} %shard_map.78.mine), channel_id=1, source_target_pairs={{0,8},{8,0},{1,9},{9,1},{2,10},{10,2},{3,11},{11,3},{4,12},{12,4},... | collective-permute-start | bytes 98312 | tf_op jit(solution)/shard_map/ppermute | solution.py:246
  88.8 8.9 %all-to-all-start.1 = ((f32[4,2,32,128]{3,2,1,0:T(8,128)}), f32[4,2,32,128]{3,2,1,0:T(8,128)S(1)}, u32[]{:S(2)}, u32[]{:S(2)}) async-start(f32[4,2,32,128]{3,2,1,0:T(8,128)} %shard_map.80), calls=%async_computation.1 | async-start | bytes 262144 | tf_op jit(solution)/shard_map/all_to_all | solution.py:251
